TPU v7x, 512 devices: a whole 4x8x8 slice. The times are simulated.
512 devices in a mesh: qrow: 16 (over z_lo, y), kcol: 32 (over z_hi, x, core).
Axes of the slice: x: 4, y: 8, z: 8 (z_hi: 4, z_lo: 2; z = z_hi * 2 + z_lo), core: 2. Of those that a mesh axis runs over, the one named last changes fastest.
Arguments:
- queries: bfloat16 [32768, 512], P(('qrow', 'kcol')), may hold values from -6 to 6
- keys: bfloat16 [32768, 128], P(('kcol', 'qrow')), may hold values from -6 to 6
- values: bfloat16 [32768, 128], P(('kcol', 'qrow')), may hold values from -6 to 6
- block_mask: int32 [256, 256], replicated, may hold values from 0 to 1, as said below
Outputs:
- attended: float32 [32768, 512], P(('qrow', 'kcol'))
Inputs may be any that keep to these rules, and one draw needn't show every extreme that they name: block_mask[a, b] is 1 only where b <= a, and always where 0 <= a - b < 3.
All inputs are finite; a program needn't handle non-finite values.
Results may differ from a plain program's by a relative error of at most 0.0022.
Values may be sent and summed in bfloat16 or wider, within the bound.
No kernel may reach another device: no remote copies, remote signals or barrier semaphores. Data moves between devices by JAX's collectives and lax.ppermute only.
A program may use at most 64 MiB of HBM per device.

v0:
```python
import math

import jax
import jax.numpy as jnp
from jax import lax
from jax.sharding import PartitionSpec as P

H = 4
DH = 128
BLOCK = 128


NEG_FILL = -1e30


def sent_together(arrays, axis, dim, along):
    widths = [a.shape[along] for a in arrays]
    both = jnp.concatenate(arrays, axis=along)
    result = lax.all_gather(both, axis, axis=dim, tiled=True)
    return tuple(jnp.split(result, [sum(widths[:k]) for k in range(1, len(widths))], axis=along))


def joined_along(parts, dim):
    dims = list(parts.shape[1:])
    dims[dim] *= parts.shape[0]
    return jnp.moveaxis(parts, 0, dim).reshape(dims)


def from_everyone(shard, axis):
    copies = jnp.broadcast_to(shard, (lax.axis_size(axis), *shard.shape))
    return lax.all_to_all(copies, axis, split_axis=0, concat_axis=0, tiled=True)


def gathered_copies(shard, axis, dim):
    return joined_along(from_everyone(shard, axis), dim)


def sent_together_2(arrays, axis, split_dim, concat_dim, along):
    widths = [a.shape[along] for a in arrays]
    both = jnp.concatenate(arrays, axis=along)
    result = lax.all_to_all(both, axis, split_axis=split_dim, concat_axis=concat_dim, tiled=True)
    return tuple(jnp.split(result, [sum(widths[:k]) for k in range(1, len(widths))], axis=along))


def shards(queries, keys, values, block_mask):
    inv_root = 1.0 / math.sqrt(DH)
    tok_count = queries.shape[0]
    col_count = lax.axis_size("kcol")
    query_tile = tok_count * col_count
    key_tile, value_tile = sent_together((keys, values), "qrow", 0, 1)
    key_width = key_tile.shape[0]
    block_count = key_width // BLOCK
    value_blocks = value_tile.reshape(block_count, BLOCK, DH)
    query_first = lax.axis_index("qrow") * query_tile
    key_first = lax.axis_index("kcol") * key_width
    tile_mask = lax.dynamic_slice(
        block_mask, (query_first // BLOCK, key_first // BLOCK), (query_tile // BLOCK, block_count)
    )
    column_mask = jnp.repeat(tile_mask, BLOCK, 1)
    key_pos = key_first + jnp.arange(key_width, dtype=jnp.int32)
    query_piece = gathered_copies(queries, "kcol", 0)
    row_count = query_piece.shape[0]
    part_rows = math.gcd(row_count, 512)
    part_count = row_count // part_rows
    stacked = query_piece.reshape(part_count, part_rows, H, DH)

    def one_part(index):
        start = index * part_rows
        query_heads = lax.dynamic_index_in_dim(stacked, index, 0, keepdims=False)
        scores = (
            jnp.einsum("rhd,kd->hrk", query_heads, key_tile, preferred_element_type=jnp.float32)
            * inv_root
        )
        local_rows = start + jnp.arange(part_rows, dtype=jnp.int32)
        listed = jnp.take(column_mask, local_rows // BLOCK, axis=0) == 1
        permitted = listed & (key_pos[None, :] <= (query_first + local_rows)[:, None])
        permitted = permitted.reshape(part_rows, block_count, BLOCK)
        scores = scores.reshape(H, part_rows, block_count, BLOCK)
        scores = jnp.where(permitted[None], scores, NEG_FILL)
        block_top = jnp.max(scores, axis=3)
        weights = jnp.where(permitted[None], jnp.exp(scores - block_top[..., None]), 0.0).astype(
            jnp.bfloat16
        )
        block_mass = jnp.sum(weights.astype(jnp.float32), axis=3)
        block_out = jnp.einsum(
            "hrkb,kbd->hrkd", weights, value_blocks, preferred_element_type=jnp.float32
        )
        row_top = jnp.max(block_top, axis=2)
        factor = jnp.exp(block_top - row_top[..., None])
        mixed = jnp.sum(block_out * factor[..., None], axis=2)
        row_mass = jnp.sum(block_mass * factor, axis=2)
        mixed = jnp.transpose(mixed, (1, 0, 2))
        return (mixed.reshape(part_rows, H * DH), row_top.T, row_mass.T)

    mixed_all, top_all, mass_all = lax.map(one_part, jnp.arange(part_count, dtype=jnp.int32))
    outputs = mixed_all.reshape(row_count, H * DH)
    highest = top_all.reshape(row_count, H)
    masses = mass_all.reshape(row_count, H)
    outputs, highest, masses = (outputs, highest, masses)
    received = sent_together_2((outputs, highest, masses), "kcol", 0, 0, 1)
    partial_out = received[0].reshape(col_count, tok_count, H, DH)
    partial_top = received[1].reshape(col_count, tok_count, H)
    partial_mass = received[2].reshape(col_count, tok_count, H)
    overall = jnp.max(partial_top, axis=0)
    factor = jnp.exp(partial_top - overall[None])
    denominator = jnp.sum(factor * partial_mass, axis=0)
    numerator = jnp.sum(factor[..., None] * partial_out, axis=0)
    result = numerator / denominator[..., None]
    return result.reshape(tok_count, H * DH)


def solution(mesh):
    placed = (P(("qrow", "kcol"), None), P(("kcol", "qrow"), None), P(("kcol", "qrow"), None), P())
    return jax.shard_map(
        shards, mesh=mesh, in_specs=placed, out_specs=P(("qrow", "kcol"), None), check_vma=False
    )
```

profile of v0, /device:TPU:56, one launch (start us, length us, event | category | flops | bytes accessed | tf_op | source)
XLA Modules:
  0.0 324.9 jit_solution(15319265708297880154)
XLA Ops:
  0.0 2.4 broadcast_in_dim.85
  2.4 13.2 %all-to-all-start = ((bf16[32,64,512]{2,1,0:T(8,128)(2,1)}), bf16[32,64,512]{2,1,0:T(8,128)(2,1)S(1)}, u32[]{:S(2)}, u32[]{:S(2)}) async-start(bf16[32,64,512]{2,1,0:T(8,128)(2,1)} %broadcast_in_dim.85), calls=%async_computation | async-start | bytes 4194304 | tf_op jit(solution)/shard_map/all_to_all | solution.py:31
  16.5 34.5 %all_gather.3 = bf16[1024,256]{1,0:T(8,128)(2,1)S(1)} all-gather(bf16[64,256]{1,0:T(8,128)(2,1)S(1)} %pad_maximum_fusion.1), channel_id=1, replica_groups=mesh['qrow'=16,'kcol'=32] {'qrow'}, dimensions={0}, use_global_device_ids=true | all-gather | bytes 557056 | tf_op jit(solution)/shard_map/all_gather | solution.py:19
  51.1 18.9 %all-to-all-done = bf16[32,64,512]{2,1,0:T(8,128)(2,1)S(1)} async-done(((bf16[32,64,512]{2,1,0:T(8,128)(2,1)}), bf16[32,64,512]{2,1,0:T(8,128)(2,1)S(1)}, u32[]{:S(2)}, u32[]{:S(2)}) %all-to-all-start) | async-done | bytes 2097184 | tf_op jit(solution)/shard_map/all_to_all | solution.py:31
  69.9 2.1 reshape_reshape.3
  72.0 108.1 %while.17 = (s32[]{:T(128)}, f32[4,512,512]{2,1,0:T(8,128)}, f32[4,512,4]{1,2,0:T(4,128)S(1)}, f32[4,512,4]{1,2,0:T(4,128)S(1)}, s32[4]{0:T(128)S(1)}, /*index=5...) while((s32[]{:T(128)}, f32[4,512,512]{2,1,0:T(8,128)}, ...), condition=%wide.region_6.7_spmd.clone, body=%wide.region_0.6_spmd.clone.sunk | while | flops 1119654400 | bytes 60582128 | solution.py:95
  76.6 1.9 gather_fusion
  79.6 2.6 fusion.31
  84.3 2.3 fusion.34
  86.5 5.3 %convert_reduce_fusion.2 = f32[4,512,8]{1,0,2:T(4,128)S(1)} fusion(f32[4,512,8]{1,0,2:T(4,128)S(1)} %fusion.34, pred[512,8,128]{2,0,1:T(8,128)(4,1)S(1)} %copy.83, f32[512,4,1024]{2,0,1:T(8,128)S(1)} %get-tuple-element.324), kind=kLoop, calls=%fused_computation.8.clone.1 | loop fusion | flops 14663680 | bytes 9043968 | tf_op jit(solution)/shard_map/while/body/eval_jaxpr/reduce_sum | solution.py:84
  91.9 5.3 %fusion.35 = f32[4,512,128]{2,1,0:T(8,128)S(1)} fusion(f32[4,512,8]{1,0,2:T(4,128)S(1)} %get-tuple-element.326, bf16[8,128,128]{2,1,0:T(8,128)(2,1)S(1)} %get-tuple-element.368, f32[4,512,8]{1,0,2:T(4,128)S(1)} %fusion.34, pred[512,8,128]{2,0,1:T(8,128)(4,1)S(1)} %copy.83, f32[512,4,1024]{2,0,1:T(8,128)S(1)} %get-tuple-element.324), kind=kOutput, calls=%fused_computation.5.clone.1 | convolution fusion | flops 551288832 | bytes 10354688 | tf_op jit(solution)/shard_map/while/body/eval_jaxpr/hrkb,kbd->hrkd/dot_general | solution.py:85
  103.6 1.9 gather_fusion
  106.6 2.6 fusion.31
  111.3 2.3 fusion.34
  113.6 5.3 %convert_reduce_fusion.2 = f32[4,512,8]{1,0,2:T(4,128)S(1)} fusion(f32[4,512,8]{1,0,2:T(4,128)S(1)} %fusion.34, pred[512,8,128]{2,0,1:T(8,128)(4,1)S(1)} %copy.83, f32[512,4,1024]{2,0,1:T(8,128)S(1)} %get-tuple-element.324), kind=kLoop, calls=%fused_computation.8.clone.1 | loop fusion | flops 14663680 | bytes 9043968 | tf_op jit(solution)/shard_map/while/body/eval_jaxpr/reduce_sum | solution.py:84
  118.9 5.3 %fusion.35 = f32[4,512,128]{2,1,0:T(8,128)S(1)} fusion(f32[4,512,8]{1,0,2:T(4,128)S(1)} %get-tuple-element.326, bf16[8,128,128]{2,1,0:T(8,128)(2,1)S(1)} %get-tuple-element.368, f32[4,512,8]{1,0,2:T(4,128)S(1)} %fusion.34, pred[512,8,128]{2,0,1:T(8,128)(4,1)S(1)} %copy.83, f32[512,4,1024]{2,0,1:T(8,128)S(1)} %get-tuple-element.324), kind=kOutput, calls=%fused_computation.5.clone.1 | convolution fusion | flops 551288832 | bytes 10354688 | tf_op jit(solution)/shard_map/while/body/eval_jaxpr/hrkb,kbd->hrkd/dot_general | solution.py:85
  130.7 1.9 gather_fusion
  133.6 2.6 fusion.31
  138.3 2.3 fusion.34
  140.6 5.3 %convert_reduce_fusion.2 = f32[4,512,8]{1,0,2:T(4,128)S(1)} fusion(f32[4,512,8]{1,0,2:T(4,128)S(1)} %fusion.34, pred[512,8,128]{2,0,1:T(8,128)(4,1)S(1)} %copy.83, f32[512,4,1024]{2,0,1:T(8,128)S(1)} %get-tuple-element.324), kind=kLoop, calls=%fused_computation.8.clone.1 | loop fusion | flops 14663680 | bytes 9043968 | tf_op jit(solution)/shard_map/while/body/eval_jaxpr/reduce_sum | solution.py:84
  146.0 5.3 %fusion.35 = f32[4,512,128]{2,1,0:T(8,128)S(1)} fusion(f32[4,512,8]{1,0,2:T(4,128)S(1)} %get-tuple-element.326, bf16[8,128,128]{2,1,0:T(8,128)(2,1)S(1)} %get-tuple-element.368, f32[4,512,8]{1,0,2:T(4,128)S(1)} %fusion.34, pred[512,8,128]{2,0,1:T(8,128)(4,1)S(1)} %copy.83, f32[512,4,1024]{2,0,1:T(8,128)S(1)} %get-tuple-element.324), kind=kOutput, calls=%fused_computation.5.clone.1 | convolution fusion | flops 551288832 | bytes 10354688 | tf_op jit(solution)/shard_map/while/body/eval_jaxpr/hrkb,kbd->hrkd/dot_general | solution.py:85
  157.7 1.9 gather_fusion
  160.6 2.6 fusion.31
  163.5 1.9 fusion.33
  165.3 2.3 fusion.34
  167.6 5.3 %convert_reduce_fusion.2 = f32[4,512,8]{1,0,2:T(4,128)S(1)} fusion(f32[4,512,8]{1,0,2:T(4,128)S(1)} %fusion.34, pred[512,8,128]{2,0,1:T(8,128)(4,1)S(1)} %copy.83, f32[512,4,1024]{2,0,1:T(8,128)S(1)} %get-tuple-element.324), kind=kLoop, calls=%fused_computation.8.clone.1 | loop fusion | flops 14663680 | bytes 9043968 | tf_op jit(solution)/shard_map/while/body/eval_jaxpr/reduce_sum | solution.py:84
  173.0 5.3 %fusion.35 = f32[4,512,128]{2,1,0:T(8,128)S(1)} fusion(f32[4,512,8]{1,0,2:T(4,128)S(1)} %get-tuple-element.326, bf16[8,128,128]{2,1,0:T(8,128)(2,1)S(1)} %get-tuple-element.368, f32[4,512,8]{1,0,2:T(4,128)S(1)} %fusion.34, pred[512,8,128]{2,0,1:T(8,128)(4,1)S(1)} %copy.83, f32[512,4,1024]{2,0,1:T(8,128)S(1)} %get-tuple-element.324), kind=kOutput, calls=%fused_computation.5.clone.1 | convolution fusion | flops 551288832 | bytes 10354688 | tf_op jit(solution)/shard_map/while/body/eval_jaxpr/hrkb,kbd->hrkd/dot_general | solution.py:85
  180.8 3.0 pad_maximum_fusion
  183.8 125.3 %all_to_all.14 = f32[32,64,520]{2,1,0:T(8,128)S(1)} all-to-all(f32[32,64,520]{2,1,0:T(8,128)S(1)} %pad_maximum_fusion), channel_id=1, replica_groups=mesh['qrow'=16,'kcol'=32] {'kcol'}, dimensions={0} | all-to-all | bytes 8519680 | tf_op jit(solution)/shard_map/all_to_all | solution.py:41
  309.4 3.0 split.23
  314.2 5.2 %reshape.166 = f32[32,64,4,128]{3,2,1,0:T(4,128)} reshape(f32[2048,512]{1,0:T(8,128)} %split.23) | data formatting | bytes 8388608 | tf_op jit(solution)/shard_map/reshape | solution.py:101
  319.6 4.4 %multiply_reduce_fusion.1 = f32[64,4,128]{2,1,0:T(4,128)S(1)} fusion(f32[32,64,4,128]{3,2,1,0:T(4,128)} %reshape.166, f32[32,64,4]{2,1,0:T(8,128)S(1)} %subtract_exponential_fusion.1), kind=kLoop, calls=%fused_computation.49 | loop fusion | flops 2064384 | bytes 4358144 | tf_op jit(solution)/shard_map/reduce_sum | solution.py:107
  (96 shorter events, 30.7 us)
Async XLA Ops:
  0.0 16.5 %copy-start.1 = (bf16[64,128]{1,0:T(8,128)(2,1)S(1)}, bf16[64,128]{1,0:T(8,128)(2,1)}, u32[]{:S(2)}) copy-start(bf16[64,128]{1,0:T(8,128)(2,1)} %param.8) | copy-start | bytes 49156
  0.0 16.5 %copy-start.2 = (bf16[64,128]{1,0:T(8,128)(2,1)S(1)}, bf16[64,128]{1,0:T(8,128)(2,1)}, u32[]{:S(2)}) copy-start(bf16[64,128]{1,0:T(8,128)(2,1)} %param.7) | copy-start | bytes 49156
  2.4 67.5 %all-to-all-start = ((bf16[32,64,512]{2,1,0:T(8,128)(2,1)}), bf16[32,64,512]{2,1,0:T(8,128)(2,1)S(1)}, u32[]{:S(2)}, u32[]{:S(2)}) async-start(bf16[32,64,512]{2,1,0:T(8,128)(2,1)} %broadcast_in_dim.85), calls=%async_computation | async-start | bytes 4194304 | tf_op jit(solution)/shard_map/all_to_all | solution.py:31
  309.1 3.6 %copy-start = (f32[32,64,520]{2,1,0:T(8,128)}, f32[32,64,520]{2,1,0:T(8,128)S(1)}, u32[]{:S(2)}) copy-start(f32[32,64,520]{2,1,0:T(8,128)S(1)} %all_to_all.14) | copy-start | bytes 12779524
where the time goes:
time: 328 us; the launch traced here: 325 us
  blocking collectives  160 us (49%)
  other arithmetic  52.5 us (16%)
  local copies, waits for them, and re-layouts  41 us (12%)
  matrix products  28.7 us (9%)
  waiting for transfers between devices  18.9 us (6%)
  starting transfers between devices  13.2 us (4%)
  loops' own time  10.7 us (3%)
    all_to_all x1, blocking collectives, sent_together_2(): lax.all_to_all(both, axis, split_axis=split_dim, concat_axis=concat_dim,...  125 us
    all_gather x1, blocking collectives, sent_together(): result = lax.all_gather(both, axis, axis=dim, tiled=True)  34.5 us
    reduce_sum x4, other arithmetic, one_part(): block_mass = jnp.sum(weights.astype(jnp.float32), axis=3)  21.3 us
    dot_general x4, matrix products, one_part(): jnp.einsum('hrkb,kbd->hrkd', weights, value_blocks, preferred_element_typ...  21.2 us
    all_to_all x1, waiting for transfers between devices, from_everyone(): return lax.all_to_all(copies, axis, split_axis=0, concat_axis=0, tiled=True)  18.9 us
    all_to_all x1, starting transfers between devices, from_everyone(): return lax.all_to_all(copies, axis, split_axis=0, concat_axis=0, tiled=True)  13.2 us
    and x8, other arithmetic, one_part(): listed & (key_pos[None, :] <= (query_first + local_rows)[:, None])  12.5 us
    another operation x1, loops' own time, shards(): lax.map(one_part, jnp.arange(part_count, dtype=jnp.int32))  10.7 us
  transfers between devices with their start and end apart: 1, of which 1 were waited for; matrix products, arithmetic and copies ran while one was open for 0% of the time, Pallas kernels for 0%

commit v1 on v0

v1 whole, which is shorter than its diff:
```python
import functools
import math

import jax
import jax.numpy as jnp
from jax import lax
from jax.experimental import pallas as pl
from jax.experimental.pallas import tpu as pltpu
from jax.sharding import Mesh
from jax.sharding import PartitionSpec as P

H = 4
DH = 128
BLOCK = 128
ROWS = 64
COLS = H * ROWS
NEG_FILL = -1e30
EXP2_SCALE = math.log2(math.e) / math.sqrt(DH)

AXES = ("zl", "yh", "yl", "zh", "x", "core")
SIZES = (2, 4, 2, 4, 4, 2)
Q_AXES = ("zl", "x", "core")
KV_AXES = ("zh", "yh", "yl")
N_OWN = 16
N_QB = N_OWN // 2
N_KB = 16
N_PAIR = N_QB * N_KB
EXT = DH + 16

F32 = jnp.float32
BF16 = jnp.bfloat16


def plan_kernel(table_ref, pairs_ref):
    yh, yl = lax.axis_index("yh"), lax.axis_index("yl")
    zh, x, zl = lax.axis_index("zh"), lax.axis_index("x"), lax.axis_index("zl")
    core = lax.axis_index("core")
    q_base = (yh * 2 + yl) * 16 + zh * 4
    k_base = x * 16 + core * 8 + zl * 4

    def one(i, counts):
        full, diag = counts
        kb, qb = i // N_QB, i % N_QB
        key_block = (kb // 4) * 64 + k_base + kb % 4
        query_block = (qb // 4) * 128 + q_base + qb % 4
        listed = (table_ref[qb, key_block] == 1) & (key_block <= query_block)
        on_diag = key_block == query_block

        @pl.when(listed & jnp.logical_not(on_diag))
        def _():
            pairs_ref[2 + full] = i

        @pl.when(listed & on_diag)
        def _():
            pairs_ref[N_PAIR + 1 - diag] = i

        full = full + jnp.where(listed & jnp.logical_not(on_diag), 1, 0)
        diag = diag + jnp.where(listed & on_diag, 1, 0)
        return full, diag

    full, diag = lax.fori_loop(0, N_PAIR, one, (jnp.int32(0), jnp.int32(0)))
    pairs_ref[0] = full
    pairs_ref[1] = diag


def split3(x):
    hi = x.astype(BF16)
    rest = x - hi.astype(F32)
    mid = rest.astype(BF16)
    low = (rest - mid.astype(F32)).astype(BF16)
    return hi, mid, low


def attend_kernel(pairs_ref, q_ref, kv_ref, out_ref, vt_ref, acc_ref, top_ref, *, unroll):
    ones = jnp.ones((EXT - DH, BLOCK), BF16)
    for b in range(N_KB):
        vt_ref[b, :DH, :] = kv_ref[b, :, DH:].T
        vt_ref[b, DH:, :] = ones
    acc_ref[...] = jnp.zeros_like(acc_ref)
    top_ref[...] = jnp.full_like(top_ref, NEG_FILL)

    def units(entries, diagonal):
        work = []
        for entry in entries:
            kb, qb = entry // N_QB, entry % N_QB
            for half in range(2):
                work.append((kb, 2 * qb + half, half))
        scores = [
            jnp.dot(kv_ref[kb, :, :DH], q_ref[own], preferred_element_type=F32)
            for kb, own, _ in work
        ]
        if diagonal:
            key_at = lax.broadcasted_iota(jnp.int32, (BLOCK, COLS), 0)
            row_at = lax.broadcasted_iota(jnp.int32, (BLOCK, COLS), 1) % ROWS
            scores = [
                jnp.where(key_at <= row_at + half * ROWS, s, NEG_FILL)
                for s, (_, _, half) in zip(scores, work)
            ]
        tops = [jnp.max(s, axis=0, keepdims=True) for s in scores]
        weights = [
            jnp.exp2((s - t) * EXP2_SCALE).astype(BF16) for s, t in zip(scores, tops)
        ]
        parts = [
            jnp.dot(vt_ref[kb], w, preferred_element_type=F32)
            for w, (kb, _, _) in zip(weights, work)
        ]
        for part, top, (_, own, _) in zip(parts, tops, work):
            before = top_ref[own]
            after = jnp.maximum(before, top)
            keep = jnp.exp2((before - after) * EXP2_SCALE)
            take = jnp.exp2((top - after) * EXP2_SCALE)
            acc_ref[own] = acc_ref[own] * keep + part * take
            top_ref[own] = after

    full, diag = pairs_ref[0], pairs_ref[1]
    rounds = full // unroll

    def several(i, _):
        units([pairs_ref[2 + i * unroll + k] for k in range(unroll)], False)
        return 0

    def single(i, _):
        units([pairs_ref[2 + rounds * unroll + i]], False)
        return 0

    def on_diagonal(i, _):
        units([pairs_ref[N_PAIR + 1 - i]], True)
        return 0

    lax.fori_loop(0, rounds, several, 0)
    lax.fori_loop(0, full - rounds * unroll, single, 0)
    lax.fori_loop(0, diag, on_diagonal, 0)

    def finish(own, _):
        out_ref[own, :DH, :] = acc_ref[own, :DH, :].astype(BF16)
        mass = split3(acc_ref[own, DH : DH + 1, :])
        top = split3(top_ref[own])
        fill = jnp.zeros((EXT - DH - 6, COLS), BF16)
        out_ref[own, DH:, :] = jnp.concatenate((*mass, *top, fill), axis=0)
        return 0

    lax.fori_loop(0, N_OWN, finish, 0)


def merge_kernel(parts_ref, out_ref):
    def stat(own, at):
        pieces = parts_ref[own, DH:, :].astype(F32)
        return pieces[at : at + 1] + pieces[at + 1 : at + 2] + pieces[at + 2 : at + 3]

    tops = [stat(own, 3) for own in range(N_OWN)]
    highest = functools.reduce(jnp.maximum, tops)
    factors = [jnp.exp2((t - highest) * EXP2_SCALE) for t in tops]
    total = sum(f * stat(own, 0) for own, f in enumerate(factors))
    mixed = sum(f * parts_ref[own, :DH, :].astype(F32) for own, f in enumerate(factors))
    turned = (mixed / total).T
    for h in range(H):
        out_ref[:, h * DH : (h + 1) * DH] = turned[h * ROWS : (h + 1) * ROWS, :]


VMEM = pl.BlockSpec(memory_space=pltpu.VMEM)
SMEM = pl.BlockSpec(memory_space=pltpu.SMEM)


def from_everyone(shard, axes, count):
    copies = jnp.broadcast_to(shard[None], (count, *shard.shape))
    return lax.all_to_all(copies, axes, split_axis=0, concat_axis=0, tiled=True)


def shards(queries, keys, values, block_mask):
    kv = from_everyone(jnp.concatenate((keys, values), axis=1), KV_AXES, 2 * N_KB)
    kv = kv.reshape(N_KB, BLOCK, 2 * DH)

    turned = queries.reshape(ROWS, H, DH).transpose(2, 1, 0).reshape(DH, COLS)
    gathered = from_everyone(turned, Q_AXES, N_OWN)

    line = (lax.axis_index("yh") * 2 + lax.axis_index("yl")) * 4 + lax.axis_index("zh")
    table = lax.dynamic_index_in_dim(
        block_mask.reshape(2, 32, 4, 256), line, 1, keepdims=False
    ).reshape(N_QB, 256)
    pairs = pl.pallas_call(
        plan_kernel,
        out_shape=jax.ShapeDtypeStruct((N_PAIR + 2,), jnp.int32),
        in_specs=[SMEM],
        out_specs=SMEM,
        name="plan",
    )(table)

    parts = pl.pallas_call(
        functools.partial(attend_kernel, unroll=2),
        out_shape=jax.ShapeDtypeStruct((N_OWN, EXT, COLS), BF16),
        in_specs=[SMEM, VMEM, VMEM],
        out_specs=VMEM,
        scratch_shapes=[
            pltpu.VMEM((N_KB, EXT, BLOCK), BF16),
            pltpu.VMEM((N_OWN, EXT, COLS), F32),
            pltpu.VMEM((N_OWN, 1, COLS), F32),
        ],
        name="attend",
    )(pairs, gathered, kv)

    parts = lax.all_to_all(parts, Q_AXES, split_axis=0, concat_axis=0, tiled=True)
    return pl.pallas_call(
        merge_kernel,
        out_shape=jax.ShapeDtypeStruct((ROWS, H * DH), F32),
        in_specs=[VMEM],
        out_specs=VMEM,
        name="merge",
    )(parts)


def solution(mesh):
    fine = Mesh(mesh.devices.reshape(SIZES), AXES)
    by_query = P(AXES, None)
    by_key = P(("zh", "x", "core", "zl", "yh", "yl"), None)
    return jax.shard_map(
        shards,
        mesh=fine,
        in_specs=(by_query, by_key, by_key, P()),
        out_specs=by_query,
        check_vma=False,
    )
```

time: 328 us -> 110 us (0.34)
  blocking collectives: 160 us -> 23.7 us
  other arithmetic: 52.5 us -> 0.01 us
  local copies, waits for them, and re-layouts: 41 us -> 5.03 us
  matrix products: 28.7 us -> 0 us
  Pallas kernels: 0 us -> 20.4 us
  waiting for transfers between devices: 18.9 us -> 38.8 us
  loops' own time: 10.7 us -> 0 us
  starting transfers between devices: 13.2 us -> 20.9 us
    all_to_all x1, blocking collectives: 125 us -> 23.7 us  [shards(): lax.all_to_all(parts, Q_AXES, split_axis=0, concat_axis=0, tiled=True)]
    all_gather x1 -> x0, blocking collectives: 34.5 us -> none  [sent_together(): result = lax.all_gather(both, axis, axis=dim, tiled=True)]
    dot_general x8 -> x0, matrix products: 28.7 us -> none  [the longest x4 21.2 us: one_part(): jnp.einsum('hrkb,kbd->hrkd', weights, value_blocks, preferred_element_typ...]
    reduce_sum x10 -> x0, other arithmetic: 26.1 us -> none  [the longest x4 21.3 us: one_part(): block_mass = jnp.sum(weights.astype(jnp.float32), axis=3)]
    pallas_call x0 -> x3, Pallas kernels: none -> 20.4 us  [the longest x1 12.6 us: shards(): pl.pallas_call(functools.partial(attend_kernel, unroll=2), out_shape=jax....]
    all_to_all x1 -> x2, waiting for transfers between devices: 18.9 us -> 38.8 us  [from_everyone(): return lax.all_to_all(copies, axes, split_axis=0, concat_axis=0, tiled=True)]
    and x12 -> x0, other arithmetic: 12.6 us -> none  [the longest x8 12.5 us: one_part(): listed & (key_pos[None, :] <= (query_first + local_rows)[:, None])]
    another operation x1 -> x0, loops' own time: 10.7 us -> none  [shards(): lax.map(one_part, jnp.arange(part_count, dtype=jnp.int32))]
  transfers between devices with their start and end apart: 1 -> 2, of which waited for: 1 -> 2; matrix products, arithmetic and copies ran while one was open for 0% -> 1% of each run, Pallas kernels for 0% -> 5%
where the time goes in v1:
time: 110 us; the launch traced here: 109 us
  waiting for transfers between devices  38.8 us (35%)
  blocking collectives  23.7 us (22%)
  starting transfers between devices  20.9 us (19%)
  Pallas kernels  20.4 us (19%)
  local copies, waits for them, and re-layouts  5.03 us (5%)
    all_to_all x2, waiting for transfers between devices, from_everyone(): return lax.all_to_all(copies, axes, split_axis=0, concat_axis=0, tiled=True)  38.8 us
    all_to_all x1, blocking collectives, shards(): lax.all_to_all(parts, Q_AXES, split_axis=0, concat_axis=0, tiled=True)  23.7 us
    all_to_all x2, starting transfers between devices, from_everyone(): return lax.all_to_all(copies, axes, split_axis=0, concat_axis=0, tiled=True)  20.9 us
    pallas_call x1, Pallas kernels, shards(): pl.pallas_call(functools.partial(attend_kernel, unroll=2), out_shape=jax....  12.6 us
    pallas_call x1, Pallas kernels, shards(): pl.pallas_call(plan_kernel, out_shape=jax.ShapeDtypeStruct((N_PAIR + 2,),...  5.55 us
    broadcast_in_dim x3, local copies, waits for them, and re-layouts, from_everyone(): copies = jnp.broadcast_to(shard[None], (count, *shard.shape))  2.38 us
    pallas_call x1, Pallas kernels, shards(): pl.pallas_call(merge_kernel, out_shape=jax.ShapeDtypeStruct((ROWS, H * DH...  2.27 us
  transfers between devices with their start and end apart: 2, of which 2 were waited for; matrix products, arithmetic and copies ran while one was open for 1% of the time, Pallas kernels for 5%

profile of v1, /device:TPU:56, one launch (start us, length us, event | category | flops | bytes accessed | tf_op | source)
XLA Modules:
  0.0 108.9 jit_solution(5793741902826646527)
XLA Ops:
  0.0 0.9 reshape.17
  0.9 0.1 copy.11
  1.0 1.1 broadcast_in_dim.14
  2.1 0.0 copy-start.3
  2.1 0.0 copy-start.4
  2.1 6.3 %all-to-all-start = ((bf16[16,128,256]{2,1,0:T(8,128)(2,1)}), bf16[16,128,256]{2,1,0:T(8,128)(2,1)S(1)}, u32[]{:S(2)}, u32[]{:S(2)}) async-start(bf16[16,128,256]{2,1,0:T(8,128)(2,1)} %broadcast_in_dim.14), calls=%async_computation | async-start | bytes 2097152 | tf_op jit(solution)/shard_map/all_to_all | solution.py:166
  8.4 0.0 copy-done.3
  8.4 0.0 copy-done.4
  8.5 16.6 %all-to-all-done.q_ref = bf16[16,128,256]{2,1,0:T(8,128)(2,1)S(1)} async-done(((bf16[16,128,256]{2,1,0:T(8,128)(2,1)}), bf16[16,128,256]{2,1,0:T(8,128)(2,1)S(1)}, u32[]{:S(2)}, u32[]{:S(2)}) %all-to-all-start) | async-done | bytes 1048608 | tf_op jit(solution)/shard_map/all_to_all | solution.py:166
  25.0 0.0 copy-start
  25.0 1.2 %broadcast_in_dim.15 = bf16[32,64,256]{2,1,0:T(8,128)(2,1)} broadcast(bf16[64,256]{1,0:T(8,128)(2,1)S(1)} %pad_maximum_fusion), dimensions={1,2} | broadcast | bytes 1081344 | tf_op jit(solution)/shard_map/broadcast_in_dim | solution.py:165
  26.2 0.0 copy-start.2
  26.2 0.1 copy-done
  26.3 14.6 %all-to-all-start.1 = ((bf16[32,64,256]{2,1,0:T(8,128)(2,1)}), bf16[32,64,256]{2,1,0:T(8,128)(2,1)S(1)}, u32[]{:S(2)}, u32[]{:S(2)}) async-start(bf16[32,64,256]{2,1,0:T(8,128)(2,1)} %broadcast_in_dim.15), calls=%async_computation.1 | async-start | bytes 2097152 | tf_op jit(solution)/shard_map/all_to_all | solution.py:166
  40.9 0.0 copy-done.2
  41.0 0.1 reshape.15
  41.1 0.6 reshape.16.table_ref
  41.7 5.6 %plan.1.pairs_ref = s32[130]{0:T(256)} custom-call(s32[8,256]{1,0:T(8,128)} %reshape.16.table_ref), custom_call_target="tpu_custom_call" | custom-call | tf_op jit(solution)/shard_map/plan/pallas_call | solution.py:180
  47.2 22.3 %all-to-all-done.1 = bf16[32,64,256]{2,1,0:T(8,128)(2,1)S(1)} async-done(((bf16[32,64,256]{2,1,0:T(8,128)(2,1)}), bf16[32,64,256]{2,1,0:T(8,128)(2,1)S(1)}, u32[]{:S(2)}, u32[]{:S(2)}) %all-to-all-start.1) | async-done | bytes 1048608 | tf_op jit(solution)/shard_map/all_to_all | solution.py:166
  69.5 0.0 copy-start.1
  69.5 1.0 copy-done.1
  70.4 12.6 %attend.1 = bf16[16,144,256]{2,1,0:T(8,128)(2,1)} custom-call(s32[130]{0:T(256)} %plan.1.pairs_ref, bf16[16,128,256]{2,1,0:T(8,128)(2,1)} %copy-done, bf16[16,128,256]{2,1,0:T(8,128)(2,1)} %bitcast.7), custom_call_target="tpu_custom_call" | custom-call | tf_op jit(solution)/shard_map/attend/pallas_call | solution.py:188
  83.0 23.7 %all_to_all.15.parts_ref = bf16[16,144,256]{2,1,0:T(8,128)(2,1)} all-to-all(bf16[16,144,256]{2,1,0:T(8,128)(2,1)} %attend.1), channel_id=1, replica_groups=mesh['zl'=2,'yh'=4,'yl'=2,'zh'=4,'x'=4,'core'=2] {'zl','x','core'}, dimensions={0} | all-to-all | bytes 2359296 | tf_op jit(solution)/shard_map/all_to_all | solution.py:201
  106.7 2.3 %merge.1 = f32[64,512]{1,0:T(8,128)} custom-call(bf16[16,144,256]{2,1,0:T(8,128)(2,1)} %all_to_all.15.parts_ref), custom_call_target="tpu_custom_call" | custom-call | tf_op jit(solution)/shard_map/merge/pallas_call | solution.py:202
  (3 shorter events, 0.0 us)
Async XLA Ops:
  2.1 6.4 %copy-start.3 = (bf16[64,128]{1,0:T(8,128)(2,1)S(1)}, bf16[64,128]{1,0:T(8,128)(2,1)}, u32[]{:S(2)}) copy-start(bf16[64,128]{1,0:T(8,128)(2,1)} %param.6) | copy-start | bytes 49156
  2.1 6.4 %copy-start.4 = (bf16[64,128]{1,0:T(8,128)(2,1)S(1)}, bf16[64,128]{1,0:T(8,128)(2,1)}, u32[]{:S(2)}) copy-start(bf16[64,128]{1,0:T(8,128)(2,1)} %param.5) | copy-start | bytes 49156
  2.1 23.0 %all-to-all-start = ((bf16[16,128,256]{2,1,0:T(8,128)(2,1)}), bf16[16,128,256]{2,1,0:T(8,128)(2,1)S(1)}, u32[]{:S(2)}, u32[]{:S(2)}) async-start(bf16[16,128,256]{2,1,0:T(8,128)(2,1)} %broadcast_in_dim.14), calls=%async_computation | async-start | bytes 2097152 | tf_op jit(solution)/shard_map/all_to_all | solution.py:166
  25.0 1.3 %copy-start = (bf16[16,128,256]{2,1,0:T(8,128)(2,1)}, bf16[16,128,256]{2,1,0:T(8,128)(2,1)S(1)}, u32[]{:S(2)}) copy-start(bf16[16,128,256]{2,1,0:T(8,128)(2,1)S(1)} %all-to-all-done.q_ref) | copy-start | bytes 3145732
  26.2 14.7 %copy-start.2 = (s32[256,256]{1,0:T(8,128)S(1)}, s32[256,256]{1,0:T(8,128)}, u32[]{:S(2)}) copy-start(s32[256,256]{1,0:T(8,128)} %param.7) | copy-start | bytes 786436
  26.3 43.1 %all-to-all-start.1 = ((bf16[32,64,256]{2,1,0:T(8,128)(2,1)}), bf16[32,64,256]{2,1,0:T(8,128)(2,1)S(1)}, u32[]{:S(2)}, u32[]{:S(2)}) async-start(bf16[32,64,256]{2,1,0:T(8,128)(2,1)} %broadcast_in_dim.15), calls=%async_computation.1 | async-start | bytes 2097152 | tf_op jit(solution)/shard_map/all_to_all | solution.py:166
  69.5 1.0 copy-start.1

commit v2 on v1

v2 whole, which is shorter than its diff:
```python
import functools
import math

import jax
import jax.numpy as jnp
from jax import lax
from jax.experimental import pallas as pl
from jax.experimental.pallas import tpu as pltpu
from jax.sharding import Mesh
from jax.sharding import PartitionSpec as P

H = 4
DH = 128
BLOCK = 128
ROWS = 64
COLS = H * ROWS
NEG_FILL = -1e30
EXP2_SCALE = math.log2(math.e) / math.sqrt(DH)

AXES = ("zl", "yh", "yl", "zh", "x", "core")
SIZES = (2, 4, 2, 4, 4, 2)
Q_AXES = ("x", "zl")
KV_AXES = ("zh", "yh", "yl")
N_OWN = 8
N_KB = 16
N_PAIR = N_OWN * N_KB
LIST = N_PAIR + 8
EXT = DH + 16

F32 = jnp.float32
BF16 = jnp.bfloat16


def plan_kernel(table_ref, pairs_ref):
    yh, yl = lax.axis_index("yh"), lax.axis_index("yl")
    zh, x, zl = lax.axis_index("zh"), lax.axis_index("x"), lax.axis_index("zl")
    core = lax.axis_index("core")
    q_base = (yh * 2 + yl) * 16 + zh * 4
    for side in range(2):
        k_base = x * 16 + (core if side == 0 else 1 - core) * 8 + zl * 4
        full, diag = jnp.int32(0), jnp.int32(0)
        for i in range(N_PAIR):
            kb, own = i // N_OWN, i % N_OWN
            key_block = k_base + (kb // 4) * 64 + kb % 4
            query_block = q_base + (own % 2) * 128 + own // 2
            listed = table_ref[(own % 2) * 4 + own // 2, key_block]
            on_diag = jnp.where(key_block == query_block, listed, 0)
            pairs_ref[side, 2 + full] = jnp.int32(i)
            pairs_ref[side, LIST - 1 - diag] = jnp.int32(i)
            full = full + (listed - on_diag)
            diag = diag + on_diag
        pairs_ref[side, 0] = full
        pairs_ref[side, 1] = diag


def split3(x):
    hi = x.astype(BF16)
    rest = x - hi.astype(F32)
    mid = rest.astype(BF16)
    low = (rest - mid.astype(F32)).astype(BF16)
    return hi, mid, low


def attend_kernel(side, unroll, pairs_ref, q_ref, kv_ref, *refs):
    if side == 0:
        acc_ref, top_ref, vt_ref = refs
    else:
        acc_before_ref, top_before_ref, out_ref, vt_ref, acc_ref, top_ref = refs
    ones = jnp.ones((EXT - DH, BLOCK), BF16)
    for b in range(N_KB):
        vt_ref[b, :DH, :] = kv_ref[b, :, DH:].T
        vt_ref[b, DH:, :] = ones
    acc_ref[...] = jnp.zeros_like(acc_ref)
    top_ref[...] = jnp.full_like(top_ref, NEG_FILL)

    def units(entries, diagonal):
        work = [(entry // N_OWN, entry % N_OWN) for entry in entries]
        scores = [
            jnp.dot(kv_ref[kb, :, :DH], q_ref[own], preferred_element_type=F32)
            for kb, own in work
        ]
        if diagonal:
            first = lax.axis_index("core") * ROWS
            key_at = lax.broadcasted_iota(jnp.int32, (BLOCK, COLS), 0)
            row_at = lax.broadcasted_iota(jnp.int32, (BLOCK, COLS), 1) % ROWS
            scores = [jnp.where(key_at <= row_at + first, s, NEG_FILL) for s in scores]
        tops = [jnp.max(s, axis=0, keepdims=True) for s in scores]
        weights = [
            jnp.exp2((s - t) * EXP2_SCALE).astype(BF16) for s, t in zip(scores, tops)
        ]
        parts = [
            jnp.dot(vt_ref[kb], w, preferred_element_type=F32)
            for w, (kb, _) in zip(weights, work)
        ]
        for part, top, (_, own) in zip(parts, tops, work):
            before = top_ref[own]
            after = jnp.maximum(before, top)
            keep = jnp.exp2((before - after) * EXP2_SCALE)
            take = jnp.exp2((top - after) * EXP2_SCALE)
            acc_ref[own] = acc_ref[own] * keep + part * take
            top_ref[own] = after

    full, diag = pairs_ref[side, 0], pairs_ref[side, 1]
    rounds = full // unroll

    def several(i, _):
        units([pairs_ref[side, 2 + i * unroll + k] for k in range(unroll)], False)
        return 0

    def single(i, _):
        units([pairs_ref[side, 2 + rounds * unroll + i]], False)
        return 0

    def on_diagonal(i, _):
        units([pairs_ref[side, LIST - 1 - i]], True)
        return 0

    lax.fori_loop(0, rounds, several, 0)
    lax.fori_loop(0, full - rounds * unroll, single, 0)
    lax.fori_loop(0, diag, on_diagonal, 0)
    if side == 0:
        return

    def finish(own, _):
        one, two = top_ref[own], top_before_ref[own]
        top = jnp.maximum(one, two)
        acc = acc_ref[own] * jnp.exp2((one - top) * EXP2_SCALE)
        acc = acc + acc_before_ref[own] * jnp.exp2((two - top) * EXP2_SCALE)
        out_ref[own, :DH, :] = acc[:DH].astype(BF16)
        fill = jnp.zeros((EXT - DH - 6, COLS), BF16)
        pieces = (*split3(acc[DH : DH + 1]), *split3(top), fill)
        out_ref[own, DH:, :] = jnp.concatenate(pieces, axis=0)
        return 0

    lax.fori_loop(0, N_OWN, finish, 0)


def merge_kernel(parts_ref, out_ref):
    def stat(own, at):
        pieces = parts_ref[own, DH:, :].astype(F32)
        return pieces[at : at + 1] + pieces[at + 1 : at + 2] + pieces[at + 2 : at + 3]

    tops = [stat(own, 3) for own in range(N_OWN)]
    highest = functools.reduce(jnp.maximum, tops)
    factors = [jnp.exp2((t - highest) * EXP2_SCALE) for t in tops]
    total = sum(f * stat(own, 0) for own, f in enumerate(factors))
    mixed = sum(f * parts_ref[own, :DH, :].astype(F32) for own, f in enumerate(factors))
    turned = (mixed / total).T
    for h in range(H):
        out_ref[:, h * DH : (h + 1) * DH] = turned[h * ROWS : (h + 1) * ROWS, :]


VMEM = pl.BlockSpec(memory_space=pltpu.VMEM)
SMEM = pl.BlockSpec(memory_space=pltpu.SMEM)


def call(kernel, name, out_shape, in_specs, scratch=(), out_specs=VMEM, flops=0):
    return pl.pallas_call(
        kernel,
        out_shape=out_shape,
        in_specs=in_specs,
        out_specs=out_specs,
        scratch_shapes=scratch,
        compiler_params=pltpu.CompilerParams(vmem_limit_bytes=16 << 20),
        cost_estimate=pl.CostEstimate(
            flops=flops, bytes_accessed=4 << 20, transcendentals=flops // 512
        ),
        name=name,
    )


def shards(queries, keys, values, block_mask):
    kv = jnp.concatenate((keys, values), axis=1)
    kv = jnp.broadcast_to(kv[None], (2 * N_KB, ROWS, 2 * DH))
    kv = lax.all_to_all(kv, KV_AXES, split_axis=0, concat_axis=0, tiled=True)
    kv = kv.reshape(N_KB, BLOCK, 2 * DH)

    turned = queries.reshape(ROWS, H, DH).transpose(2, 1, 0).reshape(DH, COLS)
    gathered = lax.all_gather(turned, "zl", axis=0, tiled=True)
    gathered = lax.all_gather(gathered, "x", axis=0, tiled=True)
    gathered = gathered.reshape(N_OWN, DH, COLS)

    line = (lax.axis_index("yh") * 2 + lax.axis_index("yl")) * 4 + lax.axis_index("zh")
    table = lax.dynamic_index_in_dim(
        block_mask.reshape(2, 32, 4, 256), line, 1, keepdims=False
    ).reshape(N_OWN, 256)
    pairs = call(
        plan_kernel,
        "plan",
        jax.ShapeDtypeStruct((2, LIST), jnp.int32),
        [SMEM],
        out_specs=SMEM,
    )(table)

    kv, gathered, pairs = lax.optimization_barrier((kv, gathered, pairs))
    kv_other = lax.ppermute(kv, "core", [(0, 1), (1, 0)])
    acc_shape, top_shape = (N_OWN, EXT, COLS), (N_OWN, 1, COLS)
    turned_values = pltpu.VMEM((N_KB, EXT, BLOCK), BF16)
    acc, top = call(
        functools.partial(attend_kernel, 0, 2),
        "attend_own",
        (jax.ShapeDtypeStruct(acc_shape, F32), jax.ShapeDtypeStruct(top_shape, F32)),
        [SMEM, VMEM, VMEM],
        scratch=[turned_values],
        out_specs=(VMEM, VMEM),
        flops=4 << 30,
    )(pairs, gathered, kv)
    parts = call(
        functools.partial(attend_kernel, 1, 2),
        "attend_other",
        jax.ShapeDtypeStruct(acc_shape, BF16),
        [SMEM] + [VMEM] * 4,
        scratch=[turned_values, pltpu.VMEM(acc_shape, F32), pltpu.VMEM(top_shape, F32)],
        flops=4 << 30,
    )(pairs, gathered, kv_other, acc, top)

    parts = lax.all_to_all(parts, Q_AXES, split_axis=0, concat_axis=0, tiled=True)
    return call(
        merge_kernel, "merge", jax.ShapeDtypeStruct((ROWS, H * DH), F32), [VMEM]
    )(parts)


def solution(mesh):
    fine = Mesh(mesh.devices.reshape(SIZES), AXES)
    by_query = P(AXES, None)
    by_key = P(("zh", "x", "core", "zl", "yh", "yl"), None)
    return jax.shard_map(
        shards,
        mesh=fine,
        in_specs=(by_query, by_key, by_key, P()),
        out_specs=by_query,
        check_vma=False,
    )
```

time: 110 us -> 92.1 us (0.84)
  waiting for transfers between devices: 38.8 us -> 0.01 us
  blocking collectives: 23.7 us -> 52.2 us
  local copies, waits for them, and re-layouts: 5.03 us -> 1.43 us
  starting transfers between devices: 20.9 us -> 17.5 us
    all_to_all x2 -> x1, waiting for transfers between devices: 38.8 us -> 0.01 us  [shards(): kv = lax.all_to_all(kv, KV_AXES, split_axis=0, concat_axis=0, tiled=True)]
    all_gather x0 -> x2, blocking collectives: none -> 34.5 us  [the longest x1 21.4 us: shards(): gathered = lax.all_gather(turned, 'zl', axis=0, tiled=True)]
    all_to_all x1, blocking collectives: 23.7 us -> 17.7 us  [shards(): lax.all_to_all(parts, Q_AXES, split_axis=0, concat_axis=0, tiled=True)]
    all_to_all x2 -> x1, starting transfers between devices: 20.9 us -> 15.6 us  [shards(): kv = lax.all_to_all(kv, KV_AXES, split_axis=0, concat_axis=0, tiled=True)]
    ppermute x0 -> x1, starting transfers between devices: none -> 1.92 us  [shards(): kv_other = lax.ppermute(kv, 'core', [(0, 1), (1, 0)])]
    broadcast_in_dim x3 -> x1, local copies, waits for them, and re-layouts: 2.38 us -> 1.09 us  [shards(): kv = jnp.broadcast_to(kv[None], (2 * N_KB, ROWS, 2 * DH))]
    pallas_call x3 -> x4, Pallas kernels: 20.4 us -> 19.5 us  [the longest x1 7.84 us: shards(): call(functools.partial(attend_kernel, 0, 2), 'attend_own', (jax.ShapeDtyp...]
  transfers between devices with their start and end apart: 2 -> 2, of which waited for: 2 -> 0; matrix products, arithmetic and copies ran while one was open for 1% -> 0% of each run, Pallas kernels for 5% -> 12%
where the time goes in v2:
time: 92.1 us; the launch traced here: 91.4 us
  blocking collectives  52.2 us (57%)
  Pallas kernels  19.5 us (21%)
  starting transfers between devices  17.5 us (19%)
  local copies, waits for them, and re-layouts  1.43 us (2%)
    all_gather x1, blocking collectives, shards(): gathered = lax.all_gather(turned, 'zl', axis=0, tiled=True)  21.4 us
    all_to_all x1, blocking collectives, shards(): lax.all_to_all(parts, Q_AXES, split_axis=0, concat_axis=0, tiled=True)  17.7 us
    all_to_all x1, starting transfers between devices, shards(): kv = lax.all_to_all(kv, KV_AXES, split_axis=0, concat_axis=0, tiled=True)  15.6 us
    all_gather x1, blocking collectives, shards(): gathered = lax.all_gather(gathered, 'x', axis=0, tiled=True)  13.1 us
    pallas_call x1, Pallas kernels, shards(): call(functools.partial(attend_kernel, 0, 2), 'attend_own', (jax.ShapeDtyp...  7.84 us
    pallas_call x1, Pallas kernels, shards(): call(functools.partial(attend_kernel, 1, 2), 'attend_other', jax.ShapeDty...  7.7 us
    pallas_call x1, Pallas kernels, shards(): call(plan_kernel, 'plan', jax.ShapeDtypeStruct((2, LIST), jnp.int32), [SM...  3.05 us
    ppermute x1, starting transfers between devices, shards(): kv_other = lax.ppermute(kv, 'core', [(0, 1), (1, 0)])  1.92 us
  transfers between devices with their start and end apart: 2, of which 0 were waited for; matrix products, arithmetic and copies ran while one was open for 0% of the time, Pallas kernels for 12%

profile of v2, /device:TPU:56, one launch (start us, length us, event | category | flops | bytes accessed | tf_op | source)
XLA Modules:
  0.0 91.4 jit_solution(1073641155669186677)
XLA Ops:
  0.0 0.7 pad_maximum_fusion
  0.7 1.1 %broadcast_in_dim.2 = bf16[32,64,256]{2,1,0:T(8,128)(2,1)} broadcast(bf16[64,256]{1,0:T(8,128)(2,1)S(1)} %pad_maximum_fusion), dimensions={1,2} | broadcast | bytes 1081344 | tf_op jit(solution)/shard_map/broadcast_in_dim | solution.py:174
  1.8 0.0 copy-start.1
  1.8 0.0 copy-start
  1.8 15.6 %all-to-all-start = ((bf16[32,64,256]{2,1,0:T(8,128)(2,1)}), bf16[32,64,256]{2,1,0:T(8,128)(2,1)S(1)}, u32[]{:S(2)}, u32[]{:S(2)}) async-start(bf16[32,64,256]{2,1,0:T(8,128)(2,1)} %broadcast_in_dim.2), calls=%async_computation | async-start | bytes 2097152 | tf_op jit(solution)/shard_map/all_to_all | solution.py:175
  17.5 0.0 copy-done.1
  17.5 0.0 copy-done
  17.5 0.1 reshape.24
  17.7 3.1 %plan.1.pairs_ref = s32[2,136]{1,0:T(2,128)S(1)} custom-call(s32[8,256]{1,0:T(8,128)S(1)} %reshape.25.table_ref), custom_call_target="tpu_custom_call" | custom-call | bytes 4194304 | tf_op jit(solution)/shard_map/plan/pallas_call | solution.py:187
  20.7 21.4 %all_gather.6 = bf16[256,256]{0,1:T(8,128)(2,1)S(1)} all-gather(bf16[128,256]{0,1:T(8,128)(2,1)S(1)} %bitcast.12), channel_id=1, replica_groups=mesh['zl'=2,'yh'=4,'yl'=2,'zh'=4,'x'=4,'core'=2] {'zl'}, dimensions={0}, use_global_device_ids=true | all-gather | bytes 196608 | tf_op jit(solution)/shard_map/all_gather | solution.py:179
  42.1 13.1 %all_gather.7 = bf16[1024,256]{0,1:T(8,128)(2,1)S(1)} all-gather(bf16[256,256]{0,1:T(8,128)(2,1)S(1)} %all_gather.6), channel_id=1, replica_groups=mesh['zl'=2,'yh'=4,'yl'=2,'zh'=4,'x'=4,'core'=2] {'x'}, dimensions={0}, use_global_device_ids=true | all-gather | bytes 655360 | tf_op jit(solution)/shard_map/all_gather | solution.py:180
  55.2 0.2 copy.10
  55.4 0.0 all-to-all-done
  55.4 1.9 %collective-permute-start = (bf16[16,128,256]{2,1,0:T(8,128)(2,1)S(1)}, bf16[16,128,256]{2,1,0:T(8,128)(2,1)S(1)}, u32[]{:S(2)}, u32[]{:S(2)}) collective-permute-start(bf16[16,128,256]{2,1,0:T(8,128)(2,1)S(1)} %bitcast.8), channel_id=1, source_target_pairs={{0,1},{1,0},{2,3},{3,2},{4,5},{5,4},{6,7},{7,6},{8,9},{9,8},{10,11... | collective-permute-start | bytes 3145736 | tf_op jit(solution)/shard_map/ppermute | solution.py:196
  57.3 7.8 %attend_own.1 = (f32[8,144,256]{2,1,0:T(8,128)S(1)}, f32[8,1,256]{2,1,0:T(1,128)S(1)}) custom-call(s32[2,136]{1,0:T(2,128)S(1)} %plan.1.pairs_ref, bf16[8,128,256]{2,1,0:T(8,128)(2,1)S(1)} %bitcast.10, bf16[16,128,256]{2,1,0:T(8,128)(2,1)S(1)} %bitcast.9), custom_call_target="tpu_custom_call" | custom-call | flops 4294967296 | bytes 4194304 | tf_op jit(solution)/shard_map/attend_own/pallas_call | solution.py:199
  65.2 0.0 collective-permute-done.kv_ref
  65.2 7.7 %attend_other.1 = bf16[8,144,256]{2,1,0:T(8,128)(2,1)S(1)} custom-call(s32[2,136]{1,0:T(2,128)S(1)} %plan.1.pairs_ref, bf16[8,128,256]{2,1,0:T(8,128)(2,1)S(1)} %bitcast.11, bf16[16,128,256]{2,1,0:T(8,128)(2,1)S(1)} %collective-permute-done.kv_ref, f32[8,144,256]{2,1,0:T(8,128)S(1)} %get-tuple-element.13.refs_0_, f32[8,1,256]{2,1,0:T(1,128)S(1)} %get-tuple-element.14.refs_1_), custom_call_target="tpu_custom_call" | custom-call | flops 4294967296 | bytes 4194304 | tf_op jit(solution)/shard_map/attend_other/pallas_call | solution.py:208
  72.9 17.7 %all_to_all.10.parts_ref = bf16[8,144,256]{2,1,0:T(8,128)(2,1)S(1)} all-to-all(bf16[8,144,256]{2,1,0:T(8,128)(2,1)S(1)} %attend_other.1), channel_id=1, replica_groups=mesh['zl'=2,'yh'=4,'yl'=2,'zh'=4,'x'=4,'core'=2] {'x','zl'}, dimensions={0} | all-to-all | bytes 1179648 | tf_op jit(solution)/shard_map/all_to_all | solution.py:217
  90.6 0.9 merge.1
  (4 shorter events, 0.1 us)
Async XLA Ops:
  1.8 15.6 %copy-start.1 = (bf16[64,512]{1,0:T(8,128)(2,1)S(1)}, bf16[64,512]{1,0:T(8,128)(2,1)}, u32[]{:S(2)}) copy-start(bf16[64,512]{1,0:T(8,128)(2,1)} %param.4) | copy-start | bytes 196612
  1.8 15.7 %copy-start = (s32[256,256]{1,0:T(8,128)S(1)}, s32[256,256]{1,0:T(8,128)}, u32[]{:S(2)}) copy-start(s32[256,256]{1,0:T(8,128)} %param.7) | copy-start | bytes 786436
  1.8 53.6 %all-to-all-start = ((bf16[32,64,256]{2,1,0:T(8,128)(2,1)}), bf16[32,64,256]{2,1,0:T(8,128)(2,1)S(1)}, u32[]{:S(2)}, u32[]{:S(2)}) async-start(bf16[32,64,256]{2,1,0:T(8,128)(2,1)} %broadcast_in_dim.2), calls=%async_computation | async-start | bytes 2097152 | tf_op jit(solution)/shard_map/all_to_all | solution.py:175
  55.4 9.8 %collective-permute-start = (bf16[16,128,256]{2,1,0:T(8,128)(2,1)S(1)}, bf16[16,128,256]{2,1,0:T(8,128)(2,1)S(1)}, u32[]{:S(2)}, u32[]{:S(2)}) collective-permute-start(bf16[16,128,256]{2,1,0:T(8,128)(2,1)S(1)} %bitcast.8), channel_id=1, source_target_pairs={{0,1},{1,0},{2,3},{3,2},{4,5},{5,4},{6,7},{7,6},{8,9},{9,8},{10,11... | collective-permute-start | bytes 3145736 | tf_op jit(solution)/shard_map/ppermute | solution.py:196

commit v3 on v2

--- a/solution.py
+++ b/solution.py
@@ -19,7 +19,7 @@
 
 AXES = ("zl", "yh", "yl", "zh", "x", "core")
 SIZES = (2, 4, 2, 4, 4, 2)
-Q_AXES = ("x", "zl")
+Q_AXES = ("zl", "x")
 KV_AXES = ("zh", "yh", "yl")
 N_OWN = 8
 N_KB = 16
@@ -42,8 +42,8 @@
         for i in range(N_PAIR):
             kb, own = i // N_OWN, i % N_OWN
             key_block = k_base + (kb // 4) * 64 + kb % 4
-            query_block = q_base + (own % 2) * 128 + own // 2
-            listed = table_ref[(own % 2) * 4 + own // 2, key_block]
+            query_block = q_base + (own // 4) * 128 + own % 4
+            listed = table_ref[own, key_block]
             on_diag = jnp.where(key_block == query_block, listed, 0)
             pairs_ref[side, 2 + full] = jnp.int32(i)
             pairs_ref[side, LIST - 1 - diag] = jnp.int32(i)
@@ -176,8 +176,8 @@
     kv = kv.reshape(N_KB, BLOCK, 2 * DH)
 
     turned = queries.reshape(ROWS, H, DH).transpose(2, 1, 0).reshape(DH, COLS)
-    gathered = lax.all_gather(turned, "zl", axis=0, tiled=True)
-    gathered = lax.all_gather(gathered, "x", axis=0, tiled=True)
+    gathered = lax.all_gather(turned, "x", axis=0, tiled=True)
+    gathered = lax.all_gather(gathered, "zl", axis=0, tiled=True)
     gathered = gathered.reshape(N_OWN, DH, COLS)
 
     line = (lax.axis_index("yh") * 2 + lax.axis_index("yl")) * 4 + lax.axis_index("zh")

time: 92.1 us -> 88.5 us (0.961)
  blocking collectives: 52.2 us -> 47.1 us
  Pallas kernels: 19.5 us -> 21.1 us
    all_gather x2, blocking collectives: 34.5 us -> 31.1 us  [the longest x1 18.9 us: shards(): gathered = lax.all_gather(gathered, 'zl', axis=0, tiled=True)]
    all_to_all x1, blocking collectives: 17.7 us -> 16 us  [shards(): lax.all_to_all(parts, Q_AXES, split_axis=0, concat_axis=0, tiled=True)]
    pallas_call x1, Pallas kernels: 7.84 us -> 9.03 us  [shards(): call(functools.partial(attend_kernel, 0, 2), 'attend_own', (jax.ShapeDtyp...]
  transfers between devices with their start and end apart: 2 -> 2, of which waited for: 0 -> 0; matrix products, arithmetic and copies ran while one was open for 0% -> 0% of each run, Pallas kernels for 12% -> 14%
where the time goes in v3:
time: 88.5 us; the launch traced here: 88.1 us
  blocking collectives  47.1 us (53%)
  Pallas kernels  21.1 us (24%)
  starting transfers between devices  17.5 us (20%)
  local copies, waits for them, and re-layouts  1.43 us (2%)
    all_gather x1, blocking collectives, shards(): gathered = lax.all_gather(gathered, 'zl', axis=0, tiled=True)  18.9 us
    all_to_all x1, blocking collectives, shards(): lax.all_to_all(parts, Q_AXES, split_axis=0, concat_axis=0, tiled=True)  16 us
    all_to_all x1, starting transfers between devices, shards(): kv = lax.all_to_all(kv, KV_AXES, split_axis=0, concat_axis=0, tiled=True)  15.6 us
    all_gather x1, blocking collectives, shards(): gathered = lax.all_gather(turned, 'x', axis=0, tiled=True)  12.2 us
    pallas_call x1, Pallas kernels, shards(): call(functools.partial(attend_kernel, 0, 2), 'attend_own', (jax.ShapeDtyp...  9.03 us
    pallas_call x1, Pallas kernels, shards(): call(functools.partial(attend_kernel, 1, 2), 'attend_other', jax.ShapeDty...  8.17 us
    pallas_call x1, Pallas kernels, shards(): call(plan_kernel, 'plan', jax.ShapeDtypeStruct((2, LIST), jnp.int32), [SM...  3.05 us
    ppermute x1, starting transfers between devices, shards(): kv_other = lax.ppermute(kv, 'core', [(0, 1), (1, 0)])  1.92 us
  transfers between devices with their start and end apart: 2, of which 0 were waited for; matrix products, arithmetic and copies ran while one was open for 0% of the time, Pallas kernels for 14%

profile of v3, /device:TPU:56, one launch (start us, length us, event | category | flops | bytes accessed | tf_op | source)
XLA Modules:
  0.0 88.1 jit_solution(7135372991203680088)
XLA Ops:
  0.0 0.7 pad_maximum_fusion
  0.7 1.1 %broadcast_in_dim.2 = bf16[32,64,256]{2,1,0:T(8,128)(2,1)} broadcast(bf16[64,256]{1,0:T(8,128)(2,1)S(1)} %pad_maximum_fusion), dimensions={1,2} | broadcast | bytes 1081344 | tf_op jit(solution)/shard_map/broadcast_in_dim | solution.py:174
  1.8 0.0 copy-start.1
  1.8 15.6 %all-to-all-start = ((bf16[32,64,256]{2,1,0:T(8,128)(2,1)}), bf16[32,64,256]{2,1,0:T(8,128)(2,1)S(1)}, u32[]{:S(2)}, u32[]{:S(2)}) async-start(bf16[32,64,256]{2,1,0:T(8,128)(2,1)} %broadcast_in_dim.2), calls=%async_computation | async-start | bytes 2097152 | tf_op jit(solution)/shard_map/all_to_all | solution.py:175
  17.5 0.0 copy-done.1
  17.5 0.0 copy-start
  17.5 12.2 %all_gather.6 = bf16[512,256]{0,1:T(8,128)(2,1)S(1)} all-gather(bf16[128,256]{0,1:T(8,128)(2,1)S(1)} %bitcast.12), channel_id=1, replica_groups=mesh['zl'=2,'yh'=4,'yl'=2,'zh'=4,'x'=4,'core'=2] {'x'}, dimensions={0}, use_global_device_ids=true | all-gather | bytes 327680 | tf_op jit(solution)/shard_map/all_gather | solution.py:179
  29.7 18.9 %all_gather.7 = bf16[1024,256]{0,1:T(8,128)(2,1)S(1)} all-gather(bf16[512,256]{0,1:T(8,128)(2,1)S(1)} %all_gather.6), channel_id=1, replica_groups=mesh['zl'=2,'yh'=4,'yl'=2,'zh'=4,'x'=4,'core'=2] {'zl'}, dimensions={0}, use_global_device_ids=true | all-gather | bytes 786432 | tf_op jit(solution)/shard_map/all_gather | solution.py:180
  48.6 0.2 copy.10
  48.8 0.0 copy-done
  48.8 0.1 reshape.24
  49.0 3.1 %plan.1.pairs_ref = s32[2,136]{1,0:T(2,128)S(1)} custom-call(s32[8,256]{1,0:T(8,128)S(1)} %reshape.25.table_ref), custom_call_target="tpu_custom_call" | custom-call | bytes 4194304 | tf_op jit(solution)/shard_map/plan/pallas_call | solution.py:187
  52.0 0.0 all-to-all-done
  52.0 1.9 %collective-permute-start = (bf16[16,128,256]{2,1,0:T(8,128)(2,1)S(1)}, bf16[16,128,256]{2,1,0:T(8,128)(2,1)S(1)}, u32[]{:S(2)}, u32[]{:S(2)}) collective-permute-start(bf16[16,128,256]{2,1,0:T(8,128)(2,1)S(1)} %bitcast.8), channel_id=1, source_target_pairs={{0,1},{1,0},{2,3},{3,2},{4,5},{5,4},{6,7},{7,6},{8,9},{9,8},{10,11... | collective-permute-start | bytes 3145736 | tf_op jit(solution)/shard_map/ppermute | solution.py:196
  54.0 9.0 %attend_own.1 = (f32[8,144,256]{2,1,0:T(8,128)S(1)}, f32[8,1,256]{2,1,0:T(1,128)S(1)}) custom-call(s32[2,136]{1,0:T(2,128)S(1)} %plan.1.pairs_ref, bf16[8,128,256]{2,1,0:T(8,128)(2,1)S(1)} %bitcast.10, bf16[16,128,256]{2,1,0:T(8,128)(2,1)S(1)} %bitcast.9), custom_call_target="tpu_custom_call" | custom-call | flops 4294967296 | bytes 4194304 | tf_op jit(solution)/shard_map/attend_own/pallas_call | solution.py:199
  63.0 0.0 collective-permute-done.kv_ref
  63.0 8.2 %attend_other.1 = bf16[8,144,256]{2,1,0:T(8,128)(2,1)S(1)} custom-call(s32[2,136]{1,0:T(2,128)S(1)} %plan.1.pairs_ref, bf16[8,128,256]{2,1,0:T(8,128)(2,1)S(1)} %bitcast.11, bf16[16,128,256]{2,1,0:T(8,128)(2,1)S(1)} %collective-permute-done.kv_ref, f32[8,144,256]{2,1,0:T(8,128)S(1)} %get-tuple-element.13.refs_0_, f32[8,1,256]{2,1,0:T(1,128)S(1)} %get-tuple-element.14.refs_1_), custom_call_target="tpu_custom_call" | custom-call | flops 4294967296 | bytes 4194304 | tf_op jit(solution)/shard_map/attend_other/pallas_call | solution.py:208
  71.2 16.0 %all_to_all.10.parts_ref = bf16[8,144,256]{2,1,0:T(8,128)(2,1)S(1)} all-to-all(bf16[8,144,256]{2,1,0:T(8,128)(2,1)S(1)} %attend_other.1), channel_id=1, replica_groups=mesh['zl'=2,'yh'=4,'yl'=2,'zh'=4,'x'=4,'core'=2] {'zl','x'}, dimensions={0} | all-to-all | bytes 1179648 | tf_op jit(solution)/shard_map/all_to_all | solution.py:217
  87.2 0.9 merge.1
  (4 shorter events, 0.1 us)
Async XLA Ops:
  1.8 15.6 %copy-start.1 = (bf16[64,512]{1,0:T(8,128)(2,1)S(1)}, bf16[64,512]{1,0:T(8,128)(2,1)}, u32[]{:S(2)}) copy-start(bf16[64,512]{1,0:T(8,128)(2,1)} %param.4) | copy-start | bytes 196612
  1.8 50.2 %all-to-all-start = ((bf16[32,64,256]{2,1,0:T(8,128)(2,1)}), bf16[32,64,256]{2,1,0:T(8,128)(2,1)S(1)}, u32[]{:S(2)}, u32[]{:S(2)}) async-start(bf16[32,64,256]{2,1,0:T(8,128)(2,1)} %broadcast_in_dim.2), calls=%async_computation | async-start | bytes 2097152 | tf_op jit(solution)/shard_map/all_to_all | solution.py:175
  17.5 31.3 %copy-start = (s32[256,256]{1,0:T(8,128)S(1)}, s32[256,256]{1,0:T(8,128)}, u32[]{:S(2)}) copy-start(s32[256,256]{1,0:T(8,128)} %param.7) | copy-start | bytes 786436
  52.0 11.0 %collective-permute-start = (bf16[16,128,256]{2,1,0:T(8,128)(2,1)S(1)}, bf16[16,128,256]{2,1,0:T(8,128)(2,1)S(1)}, u32[]{:S(2)}, u32[]{:S(2)}) collective-permute-start(bf16[16,128,256]{2,1,0:T(8,128)(2,1)S(1)} %bitcast.8), channel_id=1, source_target_pairs={{0,1},{1,0},{2,3},{3,2},{4,5},{5,4},{6,7},{7,6},{8,9},{9,8},{10,11... | collective-permute-start | bytes 3145736 | tf_op jit(solution)/shard_map/ppermute | solution.py:196

commit v4 on v3

--- a/solution.py
+++ b/solution.py
@@ -25,6 +25,7 @@
 N_KB = 16
 N_PAIR = N_OWN * N_KB
 LIST = N_PAIR + 8
+WIDTHS = (8, 4, 2, 1)
 EXT = DH + 16
 
 F32 = jnp.float32
@@ -53,6 +54,11 @@
         pairs_ref[side, 1] = diag
 
 
+def turn_kernel(rows_ref, out_ref):
+    heads = [rows_ref[:, h * DH : (h + 1) * DH] for h in range(H)]
+    out_ref[...] = jnp.concatenate(heads, axis=0).T
+
+
 def split3(x):
     hi = x.astype(BF16)
     rest = x - hi.astype(F32)
@@ -61,7 +67,7 @@
     return hi, mid, low
 
 
-def attend_kernel(side, unroll, pairs_ref, q_ref, kv_ref, *refs):
+def attend_kernel(side, pairs_ref, q_ref, kv_ref, *refs):
     if side == 0:
         acc_ref, top_ref, vt_ref = refs
     else:
@@ -101,22 +107,20 @@
             top_ref[own] = after
 
     full, diag = pairs_ref[side, 0], pairs_ref[side, 1]
-    rounds = full // unroll
-
-    def several(i, _):
-        units([pairs_ref[side, 2 + i * unroll + k] for k in range(unroll)], False)
-        return 0
-
-    def single(i, _):
-        units([pairs_ref[side, 2 + rounds * unroll + i]], False)
-        return 0
+    done = jnp.int32(0)
+    for width in WIDTHS:
+        rounds = (full - done) // width
+
+        def several(i, start, width=width):
+            units([pairs_ref[side, 2 + start + k] for k in range(width)], False)
+            return start + width
+
+        done = lax.fori_loop(0, rounds, several, done)
 
     def on_diagonal(i, _):
         units([pairs_ref[side, LIST - 1 - i]], True)
         return 0
 
-    lax.fori_loop(0, rounds, several, 0)
-    lax.fori_loop(0, full - rounds * unroll, single, 0)
     lax.fori_loop(0, diag, on_diagonal, 0)
     if side == 0:
         return
@@ -175,11 +179,6 @@
     kv = lax.all_to_all(kv, KV_AXES, split_axis=0, concat_axis=0, tiled=True)
     kv = kv.reshape(N_KB, BLOCK, 2 * DH)
 
-    turned = queries.reshape(ROWS, H, DH).transpose(2, 1, 0).reshape(DH, COLS)
-    gathered = lax.all_gather(turned, "x", axis=0, tiled=True)
-    gathered = lax.all_gather(gathered, "zl", axis=0, tiled=True)
-    gathered = gathered.reshape(N_OWN, DH, COLS)
-
     line = (lax.axis_index("yh") * 2 + lax.axis_index("yl")) * 4 + lax.axis_index("zh")
     table = lax.dynamic_index_in_dim(
         block_mask.reshape(2, 32, 4, 256), line, 1, keepdims=False
@@ -192,12 +191,20 @@
         out_specs=SMEM,
     )(table)
 
+    turned = call(
+        turn_kernel, "turn", jax.ShapeDtypeStruct((DH, COLS), BF16), [VMEM]
+    )(queries)
+    gathered = lax.all_gather(turned, "x", axis=0, tiled=True)
+    gathered, pairs = lax.optimization_barrier((gathered, pairs))
+    gathered = lax.all_gather(gathered, "zl", axis=0, tiled=True)
+    gathered = gathered.reshape(N_OWN, DH, COLS)
+
     kv, gathered, pairs = lax.optimization_barrier((kv, gathered, pairs))
     kv_other = lax.ppermute(kv, "core", [(0, 1), (1, 0)])
     acc_shape, top_shape = (N_OWN, EXT, COLS), (N_OWN, 1, COLS)
     turned_values = pltpu.VMEM((N_KB, EXT, BLOCK), BF16)
     acc, top = call(
-        functools.partial(attend_kernel, 0, 2),
+        functools.partial(attend_kernel, 0),
         "attend_own",
         (jax.ShapeDtypeStruct(acc_shape, F32), jax.ShapeDtypeStruct(top_shape, F32)),
         [SMEM, VMEM, VMEM],
@@ -206,7 +213,7 @@
         flops=4 << 30,
     )(pairs, gathered, kv)
     parts = call(
-        functools.partial(attend_kernel, 1, 2),
+        functools.partial(attend_kernel, 1),
         "attend_other",
         jax.ShapeDtypeStruct(acc_shape, BF16),
         [SMEM] + [VMEM] * 4,

time: 88.5 us -> 77.7 us (0.88)
  Pallas kernels: 21.1 us -> 11.5 us
  blocking collectives: 47.1 us -> 46.1 us
    pallas_call x2 -> x3, Pallas kernels: 17.2 us -> 7.55 us  [the longest x1 3.82 us: shards(): call(functools.partial(attend_kernel, 1), 'attend_other', jax.ShapeDtypeS...]
    all_gather x1, blocking collectives: 18.9 us -> 15.4 us  [shards(): gathered = lax.all_gather(gathered, 'zl', axis=0, tiled=True)]
    all_to_all x1, blocking collectives: 16 us -> 18.1 us  [shards(): lax.all_to_all(parts, Q_AXES, split_axis=0, concat_axis=0, tiled=True)]
  transfers between devices with their start and end apart: 2 -> 2, of which waited for: 0 -> 0; matrix products, arithmetic and copies ran while one was open for 0% -> 0% of each run, Pallas kernels for 14% -> 9%
where the time goes in v4:
time: 77.7 us; the launch traced here: 77.2 us
  blocking collectives  46.1 us (59%)
  starting transfers between devices  17.5 us (23%)
  Pallas kernels  11.5 us (15%)
  local copies, waits for them, and re-layouts  1.2 us (2%)
    all_to_all x1, blocking collectives, shards(): lax.all_to_all(parts, Q_AXES, split_axis=0, concat_axis=0, tiled=True)  18.1 us
    all_to_all x1, starting transfers between devices, shards(): kv = lax.all_to_all(kv, KV_AXES, split_axis=0, concat_axis=0, tiled=True)  15.6 us
    all_gather x1, blocking collectives, shards(): gathered = lax.all_gather(gathered, 'zl', axis=0, tiled=True)  15.4 us
    all_gather x1, blocking collectives, shards(): gathered = lax.all_gather(turned, 'x', axis=0, tiled=True)  12.6 us
    pallas_call x1, Pallas kernels, shards(): call(functools.partial(attend_kernel, 1), 'attend_other', jax.ShapeDtypeS...  3.82 us
    pallas_call x1, Pallas kernels, shards(): call(functools.partial(attend_kernel, 0), 'attend_own', (jax.ShapeDtypeSt...  3.66 us
    pallas_call x1, Pallas kernels, shards(): call(plan_kernel, 'plan', jax.ShapeDtypeStruct((2, LIST), jnp.int32), [SM...  3.05 us
    ppermute x1, starting transfers between devices, shards(): kv_other = lax.ppermute(kv, 'core', [(0, 1), (1, 0)])  1.91 us
  transfers between devices with their start and end apart: 2, of which 0 were waited for; matrix products, arithmetic and copies ran while one was open for 0% of the time, Pallas kernels for 9%

profile of v4, /device:TPU:56, one launch (start us, length us, event | category | flops | bytes accessed | tf_op | source)
XLA Modules:
  0.0 77.2 jit_solution(8222647840326432481)
XLA Ops:
  0.0 0.7 pad_maximum_fusion
  0.7 1.1 %broadcast_in_dim.2 = bf16[32,64,256]{2,1,0:T(8,128)(2,1)} broadcast(bf16[64,256]{1,0:T(8,128)(2,1)S(1)} %pad_maximum_fusion), dimensions={1,2} | broadcast | bytes 1081344 | tf_op jit(solution)/shard_map/broadcast_in_dim | solution.py:178
  1.8 0.0 copy-start
  1.8 0.0 copy-start.1
  1.8 15.6 %all-to-all-start = ((bf16[32,64,256]{2,1,0:T(8,128)(2,1)}), bf16[32,64,256]{2,1,0:T(8,128)(2,1)S(1)}, u32[]{:S(2)}, u32[]{:S(2)}) async-start(bf16[32,64,256]{2,1,0:T(8,128)(2,1)} %broadcast_in_dim.2), calls=%async_computation | async-start | bytes 2097152 | tf_op jit(solution)/shard_map/all_to_all | solution.py:179
  17.5 0.0 copy-done
  17.5 0.1 turn.1
  17.6 0.0 copy-done.1
  17.6 0.1 reshape.15
  17.7 3.1 %plan.1.pairs_ref = s32[2,136]{1,0:T(2,128)S(1)} custom-call(s32[8,256]{1,0:T(8,128)S(1)} %reshape.16.table_ref), custom_call_target="tpu_custom_call" | custom-call | bytes 4194304 | tf_op jit(solution)/shard_map/plan/pallas_call | solution.py:186
  20.7 12.6 %all_gather.6 = bf16[512,256]{1,0:T(8,128)(2,1)S(1)} all-gather(bf16[128,256]{1,0:T(8,128)(2,1)S(1)} %turn.1), channel_id=1, replica_groups=mesh['zl'=2,'yh'=4,'yl'=2,'zh'=4,'x'=4,'core'=2] {'x'}, dimensions={0}, use_global_device_ids=true | all-gather | bytes 327680 | tf_op jit(solution)/shard_map/all_gather | solution.py:197
  33.4 15.4 %all_gather.7 = bf16[1024,256]{1,0:T(8,128)(2,1)S(1)} all-gather(bf16[512,256]{1,0:T(8,128)(2,1)S(1)} %all_gather.6), channel_id=1, replica_groups=mesh['zl'=2,'yh'=4,'yl'=2,'zh'=4,'x'=4,'core'=2] {'zl'}, dimensions={0}, use_global_device_ids=true | all-gather | bytes 786432 | tf_op jit(solution)/shard_map/all_gather | solution.py:199
  48.8 0.0 all-to-all-done
  48.8 1.9 %collective-permute-start = (bf16[16,128,256]{2,1,0:T(8,128)(2,1)S(1)}, bf16[16,128,256]{2,1,0:T(8,128)(2,1)S(1)}, u32[]{:S(2)}, u32[]{:S(2)}) collective-permute-start(bf16[16,128,256]{2,1,0:T(8,128)(2,1)S(1)} %bitcast.6), channel_id=1, source_target_pairs={{0,1},{1,0},{2,3},{3,2},{4,5},{5,4},{6,7},{7,6},{8,9},{9,8},{10,11... | collective-permute-start | bytes 3145736 | tf_op jit(solution)/shard_map/ppermute | solution.py:203
  50.7 3.7 %attend_own.1 = (f32[8,144,256]{2,1,0:T(8,128)S(1)}, f32[8,1,256]{2,1,0:T(1,128)S(1)}) custom-call(s32[2,136]{1,0:T(2,128)S(1)} %plan.1.pairs_ref, bf16[8,128,256]{2,1,0:T(8,128)(2,1)S(1)} %bitcast.8, bf16[16,128,256]{2,1,0:T(8,128)(2,1)S(1)} %bitcast.7), custom_call_target="tpu_custom_call" | custom-call | flops 4294967296 | bytes 4194304 | tf_op jit(solution)/shard_map/attend_own/pallas_call | solution.py:206
  54.4 0.0 collective-permute-done.kv_ref
  54.4 3.8 %attend_other.1 = bf16[8,144,256]{2,1,0:T(8,128)(2,1)S(1)} custom-call(s32[2,136]{1,0:T(2,128)S(1)} %plan.1.pairs_ref, bf16[8,128,256]{2,1,0:T(8,128)(2,1)S(1)} %bitcast.9, bf16[16,128,256]{2,1,0:T(8,128)(2,1)S(1)} %collective-permute-done.kv_ref, f32[8,144,256]{2,1,0:T(8,128)S(1)} %get-tuple-element.17.refs_0_, f32[8,1,256]{2,1,0:T(1,128)S(1)} %get-tuple-element.18.refs_1_), custom_call_target="tpu_custom_call" | custom-call | flops 4294967296 | bytes 4194304 | tf_op jit(solution)/shard_map/attend_other/pallas_call | solution.py:215
  58.2 18.1 %all_to_all.10.parts_ref = bf16[8,144,256]{2,1,0:T(8,128)(2,1)S(1)} all-to-all(bf16[8,144,256]{2,1,0:T(8,128)(2,1)S(1)} %attend_other.1), channel_id=1, replica_groups=mesh['zl'=2,'yh'=4,'yl'=2,'zh'=4,'x'=4,'core'=2] {'zl','x'}, dimensions={0} | all-to-all | bytes 1179648 | tf_op jit(solution)/shard_map/all_to_all | solution.py:224
  76.3 0.9 %merge.1 = f32[64,512]{1,0:T(8,128)} custom-call(bf16[8,144,256]{2,1,0:T(8,128)(2,1)S(1)} %all_to_all.10.parts_ref), custom_call_target="tpu_custom_call" | custom-call | bytes 4194304 | tf_op jit(solution)/shard_map/merge/pallas_call | solution.py:225
  (2 shorter events, 0.0 us)
Async XLA Ops:
  1.8 15.6 %copy-start = (bf16[64,512]{1,0:T(8,128)(2,1)S(1)}, bf16[64,512]{1,0:T(8,128)(2,1)}, u32[]{:S(2)}) copy-start(bf16[64,512]{1,0:T(8,128)(2,1)} %rows_ref.1) | copy-start | bytes 196612
  1.8 15.7 %copy-start.1 = (s32[256,256]{1,0:T(8,128)S(1)}, s32[256,256]{1,0:T(8,128)}, u32[]{:S(2)}) copy-start(s32[256,256]{1,0:T(8,128)} %param.7) | copy-start | bytes 786436
  1.8 46.9 %all-to-all-start = ((bf16[32,64,256]{2,1,0:T(8,128)(2,1)}), bf16[32,64,256]{2,1,0:T(8,128)(2,1)S(1)}, u32[]{:S(2)}, u32[]{:S(2)}) async-start(bf16[32,64,256]{2,1,0:T(8,128)(2,1)} %broadcast_in_dim.2), calls=%async_computation | async-start | bytes 2097152 | tf_op jit(solution)/shard_map/all_to_all | solution.py:179
  48.8 5.6 %collective-permute-start = (bf16[16,128,256]{2,1,0:T(8,128)(2,1)S(1)}, bf16[16,128,256]{2,1,0:T(8,128)(2,1)S(1)}, u32[]{:S(2)}, u32[]{:S(2)}) collective-permute-start(bf16[16,128,256]{2,1,0:T(8,128)(2,1)S(1)} %bitcast.6), channel_id=1, source_target_pairs={{0,1},{1,0},{2,3},{3,2},{4,5},{5,4},{6,7},{7,6},{8,9},{9,8},{10,11... | collective-permute-start | bytes 3145736 | tf_op jit(solution)/shard_map/ppermute | solution.py:203

commit v5 on v4

--- a/solution.py
+++ b/solution.py
@@ -25,7 +25,8 @@
 N_KB = 16
 N_PAIR = N_OWN * N_KB
 LIST = N_PAIR + 8
-WIDTHS = (8, 4, 2, 1)
+WIDTHS = (12, 4, 2, 1)
+DIAGONAL_WIDTHS = (8, 1)
 EXT = DH + 16
 
 F32 = jnp.float32
@@ -107,21 +108,19 @@
             top_ref[own] = after
 
     full, diag = pairs_ref[side, 0], pairs_ref[side, 1]
-    done = jnp.int32(0)
-    for width in WIDTHS:
-        rounds = (full - done) // width
-
-        def several(i, start, width=width):
-            units([pairs_ref[side, 2 + start + k] for k in range(width)], False)
-            return start + width
-
-        done = lax.fori_loop(0, rounds, several, done)
-
-    def on_diagonal(i, _):
-        units([pairs_ref[side, LIST - 1 - i]], True)
-        return 0
-
-    lax.fori_loop(0, diag, on_diagonal, 0)
+
+    def run(count, widths, entry_at, diagonal):
+        done = jnp.int32(0)
+        for width in widths:
+
+            def several(i, start, width=width):
+                units([entry_at(start + k) for k in range(width)], diagonal)
+                return start + width
+
+            done = lax.fori_loop(0, (count - done) // width, several, done)
+
+    run(full, WIDTHS, lambda at: pairs_ref[side, 2 + at], False)
+    run(diag, DIAGONAL_WIDTHS, lambda at: pairs_ref[side, LIST - 1 - at], True)
     if side == 0:
         return
 

time: 77.7 us -> 76.2 us (0.981)
  Pallas kernels: 11.5 us -> 10.3 us
  transfers between devices with their start and end apart: 2 -> 2, of which waited for: 0 -> 0; matrix products, arithmetic and copies ran while one was open for 0% -> 0% of each run, Pallas kernels for 9% -> 8%
where the time goes in v5:
time: 76.2 us; the launch traced here: 75.8 us
  blocking collectives  45.9 us (60%)
  starting transfers between devices  17.5 us (23%)
  Pallas kernels  10.3 us (14%)
  local copies, waits for them, and re-layouts  1.2 us (2%)
    all_to_all x1, blocking collectives, shards(): lax.all_to_all(parts, Q_AXES, split_axis=0, concat_axis=0, tiled=True)  17.9 us
    all_to_all x1, starting transfers between devices, shards(): kv = lax.all_to_all(kv, KV_AXES, split_axis=0, concat_axis=0, tiled=True)  15.6 us
    all_gather x1, blocking collectives, shards(): gathered = lax.all_gather(gathered, 'zl', axis=0, tiled=True)  15.4 us
    all_gather x1, blocking collectives, shards(): gathered = lax.all_gather(turned, 'x', axis=0, tiled=True)  12.6 us
    pallas_call x1, Pallas kernels, shards(): call(functools.partial(attend_kernel, 0), 'attend_own', (jax.ShapeDtypeSt...  3.15 us
    pallas_call x1, Pallas kernels, shards(): call(functools.partial(attend_kernel, 1), 'attend_other', jax.ShapeDtypeS...  3.13 us
    pallas_call x1, Pallas kernels, shards(): call(plan_kernel, 'plan', jax.ShapeDtypeStruct((2, LIST), jnp.int32), [SM...  3.05 us
    ppermute x1, starting transfers between devices, shards(): kv_other = lax.ppermute(kv, 'core', [(0, 1), (1, 0)])  1.91 us
  transfers between devices with their start and end apart: 2, of which 0 were waited for; matrix products, arithmetic and copies ran while one was open for 0% of the time, Pallas kernels for 8%

profile of v5, /device:TPU:56, one launch (start us, length us, event | category | flops | bytes accessed | tf_op | source)
XLA Modules:
  0.0 75.8 jit_solution(12268359039987753295)
XLA Ops:
  0.0 0.7 pad_maximum_fusion
  0.7 1.1 %broadcast_in_dim.2 = bf16[32,64,256]{2,1,0:T(8,128)(2,1)} broadcast(bf16[64,256]{1,0:T(8,128)(2,1)S(1)} %pad_maximum_fusion), dimensions={1,2} | broadcast | bytes 1081344 | tf_op jit(solution)/shard_map/broadcast_in_dim | solution.py:177
  1.8 0.0 copy-start
  1.8 0.0 copy-start.1
  1.8 15.6 %all-to-all-start = ((bf16[32,64,256]{2,1,0:T(8,128)(2,1)}), bf16[32,64,256]{2,1,0:T(8,128)(2,1)S(1)}, u32[]{:S(2)}, u32[]{:S(2)}) async-start(bf16[32,64,256]{2,1,0:T(8,128)(2,1)} %broadcast_in_dim.2), calls=%async_computation | async-start | bytes 2097152 | tf_op jit(solution)/shard_map/all_to_all | solution.py:178
  17.5 0.0 copy-done
  17.5 0.1 turn.1
  17.6 0.0 copy-done.1
  17.6 0.1 reshape.15
  17.7 3.1 %plan.1.pairs_ref = s32[2,136]{1,0:T(2,128)S(1)} custom-call(s32[8,256]{1,0:T(8,128)S(1)} %reshape.16.table_ref), custom_call_target="tpu_custom_call" | custom-call | bytes 4194304 | tf_op jit(solution)/shard_map/plan/pallas_call | solution.py:185
  20.7 12.6 %all_gather.6 = bf16[512,256]{1,0:T(8,128)(2,1)S(1)} all-gather(bf16[128,256]{1,0:T(8,128)(2,1)S(1)} %turn.1), channel_id=1, replica_groups=mesh['zl'=2,'yh'=4,'yl'=2,'zh'=4,'x'=4,'core'=2] {'x'}, dimensions={0}, use_global_device_ids=true | all-gather | bytes 327680 | tf_op jit(solution)/shard_map/all_gather | solution.py:196
  33.4 15.4 %all_gather.7 = bf16[1024,256]{1,0:T(8,128)(2,1)S(1)} all-gather(bf16[512,256]{1,0:T(8,128)(2,1)S(1)} %all_gather.6), channel_id=1, replica_groups=mesh['zl'=2,'yh'=4,'yl'=2,'zh'=4,'x'=4,'core'=2] {'zl'}, dimensions={0}, use_global_device_ids=true | all-gather | bytes 786432 | tf_op jit(solution)/shard_map/all_gather | solution.py:198
  48.8 0.0 all-to-all-done
  48.8 1.9 %collective-permute-start = (bf16[16,128,256]{2,1,0:T(8,128)(2,1)S(1)}, bf16[16,128,256]{2,1,0:T(8,128)(2,1)S(1)}, u32[]{:S(2)}, u32[]{:S(2)}) collective-permute-start(bf16[16,128,256]{2,1,0:T(8,128)(2,1)S(1)} %bitcast.6), channel_id=1, source_target_pairs={{0,1},{1,0},{2,3},{3,2},{4,5},{5,4},{6,7},{7,6},{8,9},{9,8},{10,11... | collective-permute-start | bytes 3145736 | tf_op jit(solution)/shard_map/ppermute | solution.py:202
  50.7 3.1 %attend_own.1 = (f32[8,144,256]{2,1,0:T(8,128)S(1)}, f32[8,1,256]{2,1,0:T(1,128)S(1)}) custom-call(s32[2,136]{1,0:T(2,128)S(1)} %plan.1.pairs_ref, bf16[8,128,256]{2,1,0:T(8,128)(2,1)S(1)} %bitcast.8, bf16[16,128,256]{2,1,0:T(8,128)(2,1)S(1)} %bitcast.7), custom_call_target="tpu_custom_call" | custom-call | flops 4294967296 | bytes 4194304 | tf_op jit(solution)/shard_map/attend_own/pallas_call | solution.py:205
  53.9 0.0 collective-permute-done.kv_ref
  53.9 3.1 %attend_other.1 = bf16[8,144,256]{2,1,0:T(8,128)(2,1)S(1)} custom-call(s32[2,136]{1,0:T(2,128)S(1)} %plan.1.pairs_ref, bf16[8,128,256]{2,1,0:T(8,128)(2,1)S(1)} %bitcast.9, bf16[16,128,256]{2,1,0:T(8,128)(2,1)S(1)} %collective-permute-done.kv_ref, f32[8,144,256]{2,1,0:T(8,128)S(1)} %get-tuple-element.17.refs_0_, f32[8,1,256]{2,1,0:T(1,128)S(1)} %get-tuple-element.18.refs_1_), custom_call_target="tpu_custom_call" | custom-call | flops 4294967296 | bytes 4194304 | tf_op jit(solution)/shard_map/attend_other/pallas_call | solution.py:214
  57.0 17.9 %all_to_all.10.parts_ref = bf16[8,144,256]{2,1,0:T(8,128)(2,1)S(1)} all-to-all(bf16[8,144,256]{2,1,0:T(8,128)(2,1)S(1)} %attend_other.1), channel_id=1, replica_groups=mesh['zl'=2,'yh'=4,'yl'=2,'zh'=4,'x'=4,'core'=2] {'zl','x'}, dimensions={0} | all-to-all | bytes 1179648 | tf_op jit(solution)/shard_map/all_to_all | solution.py:223
  74.9 0.9 %merge.1 = f32[64,512]{1,0:T(8,128)} custom-call(bf16[8,144,256]{2,1,0:T(8,128)(2,1)S(1)} %all_to_all.10.parts_ref), custom_call_target="tpu_custom_call" | custom-call | bytes 4194304 | tf_op jit(solution)/shard_map/merge/pallas_call | solution.py:224
  (2 shorter events, 0.0 us)
Async XLA Ops:
  1.8 15.6 %copy-start = (bf16[64,512]{1,0:T(8,128)(2,1)S(1)}, bf16[64,512]{1,0:T(8,128)(2,1)}, u32[]{:S(2)}) copy-start(bf16[64,512]{1,0:T(8,128)(2,1)} %rows_ref.1) | copy-start | bytes 196612
  1.8 15.7 %copy-start.1 = (s32[256,256]{1,0:T(8,128)S(1)}, s32[256,256]{1,0:T(8,128)}, u32[]{:S(2)}) copy-start(s32[256,256]{1,0:T(8,128)} %param.7) | copy-start | bytes 786436
  1.8 46.9 %all-to-all-start = ((bf16[32,64,256]{2,1,0:T(8,128)(2,1)}), bf16[32,64,256]{2,1,0:T(8,128)(2,1)S(1)}, u32[]{:S(2)}, u32[]{:S(2)}) async-start(bf16[32,64,256]{2,1,0:T(8,128)(2,1)} %broadcast_in_dim.2), calls=%async_computation | async-start | bytes 2097152 | tf_op jit(solution)/shard_map/all_to_all | solution.py:178
  48.8 5.1 %collective-permute-start = (bf16[16,128,256]{2,1,0:T(8,128)(2,1)S(1)}, bf16[16,128,256]{2,1,0:T(8,128)(2,1)S(1)}, u32[]{:S(2)}, u32[]{:S(2)}) collective-permute-start(bf16[16,128,256]{2,1,0:T(8,128)(2,1)S(1)} %bitcast.6), channel_id=1, source_target_pairs={{0,1},{1,0},{2,3},{3,2},{4,5},{5,4},{6,7},{7,6},{8,9},{9,8},{10,11... | collective-permute-start | bytes 3145736 | tf_op jit(solution)/shard_map/ppermute | solution.py:202

commit v6 on v5

--- a/solution.py
+++ b/solution.py
@@ -27,7 +27,7 @@
 LIST = N_PAIR + 8
 WIDTHS = (12, 4, 2, 1)
 DIAGONAL_WIDTHS = (8, 1)
-EXT = DH + 16
+EXT = DH + 8
 
 F32 = jnp.float32
 BF16 = jnp.bfloat16
@@ -77,8 +77,12 @@
     for b in range(N_KB):
         vt_ref[b, :DH, :] = kv_ref[b, :, DH:].T
         vt_ref[b, DH:, :] = ones
-    acc_ref[...] = jnp.zeros_like(acc_ref)
-    top_ref[...] = jnp.full_like(top_ref, NEG_FILL)
+    if side == 0:
+        acc_ref[...] = jnp.zeros_like(acc_ref)
+        top_ref[...] = jnp.full_like(top_ref, NEG_FILL)
+    else:
+        acc_ref[...] = acc_before_ref[...]
+        top_ref[...] = top_before_ref[...]
 
     def units(entries, diagonal):
         work = [(entry // N_OWN, entry % N_OWN) for entry in entries]
@@ -125,13 +129,10 @@
         return
 
     def finish(own, _):
-        one, two = top_ref[own], top_before_ref[own]
-        top = jnp.maximum(one, two)
-        acc = acc_ref[own] * jnp.exp2((one - top) * EXP2_SCALE)
-        acc = acc + acc_before_ref[own] * jnp.exp2((two - top) * EXP2_SCALE)
+        acc = acc_ref[own]
         out_ref[own, :DH, :] = acc[:DH].astype(BF16)
         fill = jnp.zeros((EXT - DH - 6, COLS), BF16)
-        pieces = (*split3(acc[DH : DH + 1]), *split3(top), fill)
+        pieces = (*split3(acc[DH : DH + 1]), *split3(top_ref[own]), fill)
         out_ref[own, DH:, :] = jnp.concatenate(pieces, axis=0)
         return 0
 

time: 76.2 us -> 75.6 us (level)
  blocking collectives: 45.9 us -> 47 us
  Pallas kernels: 10.3 us -> 9.32 us
    all_to_all x1, blocking collectives: 17.9 us -> 19 us  [shards(): lax.all_to_all(parts, Q_AXES, split_axis=0, concat_axis=0, tiled=True)]
where the time goes in v6:
time: 75.6 us; the launch traced here: 75.9 us
  blocking collectives  47 us (62%)
  starting transfers between devices  17.5 us (23%)
  Pallas kernels  9.32 us (12%)
  local copies, waits for them, and re-layouts  1.2 us (2%)
    all_to_all x1, blocking collectives, shards(): lax.all_to_all(parts, Q_AXES, split_axis=0, concat_axis=0, tiled=True)  19 us
    all_to_all x1, starting transfers between devices, shards(): kv = lax.all_to_all(kv, KV_AXES, split_axis=0, concat_axis=0, tiled=True)  15.6 us
    all_gather x1, blocking collectives, shards(): gathered = lax.all_gather(gathered, 'zl', axis=0, tiled=True)  15.4 us
    all_gather x1, blocking collectives, shards(): gathered = lax.all_gather(turned, 'x', axis=0, tiled=True)  12.6 us
    pallas_call x1, Pallas kernels, shards(): call(plan_kernel, 'plan', jax.ShapeDtypeStruct((2, LIST), jnp.int32), [SM...  3.05 us
    pallas_call x1, Pallas kernels, shards(): call(functools.partial(attend_kernel, 0), 'attend_own', (jax.ShapeDtypeSt...  2.82 us
    pallas_call x1, Pallas kernels, shards(): call(functools.partial(attend_kernel, 1), 'attend_other', jax.ShapeDtypeS...  2.53 us
    ppermute x1, starting transfers between devices, shards(): kv_other = lax.ppermute(kv, 'core', [(0, 1), (1, 0)])  1.91 us
  transfers between devices with their start and end apart: 2, of which 0 were waited for; matrix products, arithmetic and copies ran while one was open for 0% of the time, Pallas kernels for 8%

profile of v6, /device:TPU:56, one launch (start us, length us, event | category | flops | bytes accessed | tf_op | source)
XLA Modules:
  0.0 75.9 jit_solution(12271029214287097010)
XLA Ops:
  0.0 0.7 pad_maximum_fusion
  0.7 1.1 %broadcast_in_dim.2 = bf16[32,64,256]{2,1,0:T(8,128)(2,1)} broadcast(bf16[64,256]{1,0:T(8,128)(2,1)S(1)} %pad_maximum_fusion), dimensions={1,2} | broadcast | bytes 1081344 | tf_op jit(solution)/shard_map/broadcast_in_dim | solution.py:178
  1.8 0.0 copy-start
  1.8 0.0 copy-start.1
  1.8 15.6 %all-to-all-start = ((bf16[32,64,256]{2,1,0:T(8,128)(2,1)}), bf16[32,64,256]{2,1,0:T(8,128)(2,1)S(1)}, u32[]{:S(2)}, u32[]{:S(2)}) async-start(bf16[32,64,256]{2,1,0:T(8,128)(2,1)} %broadcast_in_dim.2), calls=%async_computation | async-start | bytes 2097152 | tf_op jit(solution)/shard_map/all_to_all | solution.py:179
  17.5 0.0 copy-done
  17.5 0.1 turn.1
  17.6 0.0 copy-done.1
  17.6 0.1 reshape.15
  17.7 3.1 %plan.1.pairs_ref = s32[2,136]{1,0:T(2,128)S(1)} custom-call(s32[8,256]{1,0:T(8,128)S(1)} %reshape.16.table_ref), custom_call_target="tpu_custom_call" | custom-call | bytes 4194304 | tf_op jit(solution)/shard_map/plan/pallas_call | solution.py:186
  20.7 12.6 %all_gather.6 = bf16[512,256]{1,0:T(8,128)(2,1)S(1)} all-gather(bf16[128,256]{1,0:T(8,128)(2,1)S(1)} %turn.1), channel_id=1, replica_groups=mesh['zl'=2,'yh'=4,'yl'=2,'zh'=4,'x'=4,'core'=2] {'x'}, dimensions={0}, use_global_device_ids=true | all-gather | bytes 327680 | tf_op jit(solution)/shard_map/all_gather | solution.py:197
  33.4 15.4 %all_gather.7 = bf16[1024,256]{1,0:T(8,128)(2,1)S(1)} all-gather(bf16[512,256]{1,0:T(8,128)(2,1)S(1)} %all_gather.6), channel_id=1, replica_groups=mesh['zl'=2,'yh'=4,'yl'=2,'zh'=4,'x'=4,'core'=2] {'zl'}, dimensions={0}, use_global_device_ids=true | all-gather | bytes 786432 | tf_op jit(solution)/shard_map/all_gather | solution.py:199
  48.8 0.0 all-to-all-done
  48.8 1.9 %collective-permute-start = (bf16[16,128,256]{2,1,0:T(8,128)(2,1)S(1)}, bf16[16,128,256]{2,1,0:T(8,128)(2,1)S(1)}, u32[]{:S(2)}, u32[]{:S(2)}) collective-permute-start(bf16[16,128,256]{2,1,0:T(8,128)(2,1)S(1)} %bitcast.6), channel_id=1, source_target_pairs={{0,1},{1,0},{2,3},{3,2},{4,5},{5,4},{6,7},{7,6},{8,9},{9,8},{10,11... | collective-permute-start | bytes 3145736 | tf_op jit(solution)/shard_map/ppermute | solution.py:203
  50.7 2.8 %attend_own.1 = (f32[8,136,256]{2,1,0:T(8,128)S(1)}, f32[8,1,256]{2,1,0:T(1,128)S(1)}) custom-call(s32[2,136]{1,0:T(2,128)S(1)} %plan.1.pairs_ref, bf16[8,128,256]{2,1,0:T(8,128)(2,1)S(1)} %bitcast.8, bf16[16,128,256]{2,1,0:T(8,128)(2,1)S(1)} %bitcast.7), custom_call_target="tpu_custom_call" | custom-call | flops 4294967296 | bytes 4194304 | tf_op jit(solution)/shard_map/attend_own/pallas_call | solution.py:206
  53.5 0.0 collective-permute-done.kv_ref
  53.5 2.5 %attend_other.1 = bf16[8,136,256]{2,1,0:T(8,128)(2,1)S(1)} custom-call(s32[2,136]{1,0:T(2,128)S(1)} %plan.1.pairs_ref, bf16[8,128,256]{2,1,0:T(8,128)(2,1)S(1)} %bitcast.9, bf16[16,128,256]{2,1,0:T(8,128)(2,1)S(1)} %collective-permute-done.kv_ref, f32[8,136,256]{2,1,0:T(8,128)S(1)} %get-tuple-element.17.refs_0_, f32[8,1,256]{2,1,0:T(1,128)S(1)} %get-tuple-element.18.refs_1_), custom_call_target="tpu_custom_call" | custom-call | flops 4294967296 | bytes 4194304 | tf_op jit(solution)/shard_map/attend_other/pallas_call | solution.py:215
  56.1 19.0 %all_to_all.10.parts_ref = bf16[8,136,256]{2,1,0:T(8,128)(2,1)S(1)} all-to-all(bf16[8,136,256]{2,1,0:T(8,128)(2,1)S(1)} %attend_other.1), channel_id=1, replica_groups=mesh['zl'=2,'yh'=4,'yl'=2,'zh'=4,'x'=4,'core'=2] {'zl','x'}, dimensions={0} | all-to-all | bytes 1114112 | tf_op jit(solution)/shard_map/all_to_all | solution.py:224
  75.1 0.9 %merge.1 = f32[64,512]{1,0:T(8,128)} custom-call(bf16[8,136,256]{2,1,0:T(8,128)(2,1)S(1)} %all_to_all.10.parts_ref), custom_call_target="tpu_custom_call" | custom-call | bytes 4194304 | tf_op jit(solution)/shard_map/merge/pallas_call | solution.py:225
  (2 shorter events, 0.0 us)
Async XLA Ops:
  1.8 15.6 %copy-start = (bf16[64,512]{1,0:T(8,128)(2,1)S(1)}, bf16[64,512]{1,0:T(8,128)(2,1)}, u32[]{:S(2)}) copy-start(bf16[64,512]{1,0:T(8,128)(2,1)} %rows_ref.1) | copy-start | bytes 196612
  1.8 15.7 %copy-start.1 = (s32[256,256]{1,0:T(8,128)S(1)}, s32[256,256]{1,0:T(8,128)}, u32[]{:S(2)}) copy-start(s32[256,256]{1,0:T(8,128)} %param.7) | copy-start | bytes 786436
  1.8 46.9 %all-to-all-start = ((bf16[32,64,256]{2,1,0:T(8,128)(2,1)}), bf16[32,64,256]{2,1,0:T(8,128)(2,1)S(1)}, u32[]{:S(2)}, u32[]{:S(2)}) async-start(bf16[32,64,256]{2,1,0:T(8,128)(2,1)} %broadcast_in_dim.2), calls=%async_computation | async-start | bytes 2097152 | tf_op jit(solution)/shard_map/all_to_all | solution.py:179
  48.8 4.7 %collective-permute-start = (bf16[16,128,256]{2,1,0:T(8,128)(2,1)S(1)}, bf16[16,128,256]{2,1,0:T(8,128)(2,1)S(1)}, u32[]{:S(2)}, u32[]{:S(2)}) collective-permute-start(bf16[16,128,256]{2,1,0:T(8,128)(2,1)S(1)} %bitcast.6), channel_id=1, source_target_pairs={{0,1},{1,0},{2,3},{3,2},{4,5},{5,4},{6,7},{7,6},{8,9},{9,8},{10,11... | collective-permute-start | bytes 3145736 | tf_op jit(solution)/shard_map/ppermute | solution.py:203

commit v7 on v6

--- a/solution.py
+++ b/solution.py
@@ -128,15 +128,12 @@
     if side == 0:
         return
 
-    def finish(own, _):
+    for own in range(N_OWN):
         acc = acc_ref[own]
         out_ref[own, :DH, :] = acc[:DH].astype(BF16)
         fill = jnp.zeros((EXT - DH - 6, COLS), BF16)
         pieces = (*split3(acc[DH : DH + 1]), *split3(top_ref[own]), fill)
         out_ref[own, DH:, :] = jnp.concatenate(pieces, axis=0)
-        return 0
-
-    lax.fori_loop(0, N_OWN, finish, 0)
 
 
 def merge_kernel(parts_ref, out_ref):

time: 75.6 us -> 75.4 us (level)
  blocking collectives: 47 us -> 45.4 us
  Pallas kernels: 9.32 us -> 10.6 us
    all_to_all x1, blocking collectives: 19 us -> 17.4 us  [shards(): lax.all_to_all(parts, Q_AXES, split_axis=0, concat_axis=0, tiled=True)]
    pallas_call x1, Pallas kernels: 2.53 us -> 3.76 us  [shards(): call(functools.partial(attend_kernel, 1), 'attend_other', jax.ShapeDtypeS...]
where the time goes in v7:
time: 75.4 us; the launch traced here: 75.6 us
  blocking collectives  45.4 us (60%)
  starting transfers between devices  17.5 us (23%)
  Pallas kernels  10.6 us (14%)
  local copies, waits for them, and re-layouts  1.2 us (2%)
    all_to_all x1, blocking collectives, shards(): lax.all_to_all(parts, Q_AXES, split_axis=0, concat_axis=0, tiled=True)  17.4 us
    all_to_all x1, starting transfers between devices, shards(): kv = lax.all_to_all(kv, KV_AXES, split_axis=0, concat_axis=0, tiled=True)  15.6 us
    all_gather x1, blocking collectives, shards(): gathered = lax.all_gather(gathered, 'zl', axis=0, tiled=True)  15.4 us
    all_gather x1, blocking collectives, shards(): gathered = lax.all_gather(turned, 'x', axis=0, tiled=True)  12.6 us
    pallas_call x1, Pallas kernels, shards(): call(functools.partial(attend_kernel, 1), 'attend_other', jax.ShapeDtypeS...  3.76 us
    pallas_call x1, Pallas kernels, shards(): call(plan_kernel, 'plan', jax.ShapeDtypeStruct((2, LIST), jnp.int32), [SM...  3.05 us
    pallas_call x1, Pallas kernels, shards(): call(functools.partial(attend_kernel, 0), 'attend_own', (jax.ShapeDtypeSt...  2.83 us
    ppermute x1, starting transfers between devices, shards(): kv_other = lax.ppermute(kv, 'core', [(0, 1), (1, 0)])  1.91 us
  transfers between devices with their start and end apart: 2, of which 0 were waited for; matrix products, arithmetic and copies ran while one was open for 0% of the time, Pallas kernels for 8%

profile of v7, /device:TPU:56, one launch (start us, length us, event | category | flops | bytes accessed | tf_op | source)
XLA Modules:
  0.0 75.6 jit_solution(2182503760795719138)
XLA Ops:
  0.0 0.7 pad_maximum_fusion
  0.7 1.1 %broadcast_in_dim.2 = bf16[32,64,256]{2,1,0:T(8,128)(2,1)} broadcast(bf16[64,256]{1,0:T(8,128)(2,1)S(1)} %pad_maximum_fusion), dimensions={1,2} | broadcast | bytes 1081344 | tf_op jit(solution)/shard_map/broadcast_in_dim | solution.py:175
  1.8 0.0 copy-start
  1.8 0.0 copy-start.1
  1.8 15.6 %all-to-all-start = ((bf16[32,64,256]{2,1,0:T(8,128)(2,1)}), bf16[32,64,256]{2,1,0:T(8,128)(2,1)S(1)}, u32[]{:S(2)}, u32[]{:S(2)}) async-start(bf16[32,64,256]{2,1,0:T(8,128)(2,1)} %broadcast_in_dim.2), calls=%async_computation | async-start | bytes 2097152 | tf_op jit(solution)/shard_map/all_to_all | solution.py:176
  17.5 0.0 copy-done
  17.5 0.1 turn.1
  17.6 0.0 copy-done.1
  17.6 0.1 reshape.15
  17.7 3.1 %plan.1.pairs_ref = s32[2,136]{1,0:T(2,128)S(1)} custom-call(s32[8,256]{1,0:T(8,128)S(1)} %reshape.16.table_ref), custom_call_target="tpu_custom_call" | custom-call | bytes 4194304 | tf_op jit(solution)/shard_map/plan/pallas_call | solution.py:183
  20.7 12.6 %all_gather.6 = bf16[512,256]{1,0:T(8,128)(2,1)S(1)} all-gather(bf16[128,256]{1,0:T(8,128)(2,1)S(1)} %turn.1), channel_id=1, replica_groups=mesh['zl'=2,'yh'=4,'yl'=2,'zh'=4,'x'=4,'core'=2] {'x'}, dimensions={0}, use_global_device_ids=true | all-gather | bytes 327680 | tf_op jit(solution)/shard_map/all_gather | solution.py:194
  33.4 15.4 %all_gather.7 = bf16[1024,256]{1,0:T(8,128)(2,1)S(1)} all-gather(bf16[512,256]{1,0:T(8,128)(2,1)S(1)} %all_gather.6), channel_id=1, replica_groups=mesh['zl'=2,'yh'=4,'yl'=2,'zh'=4,'x'=4,'core'=2] {'zl'}, dimensions={0}, use_global_device_ids=true | all-gather | bytes 786432 | tf_op jit(solution)/shard_map/all_gather | solution.py:196
  48.8 0.0 all-to-all-done
  48.8 1.9 %collective-permute-start = (bf16[16,128,256]{2,1,0:T(8,128)(2,1)S(1)}, bf16[16,128,256]{2,1,0:T(8,128)(2,1)S(1)}, u32[]{:S(2)}, u32[]{:S(2)}) collective-permute-start(bf16[16,128,256]{2,1,0:T(8,128)(2,1)S(1)} %bitcast.6), channel_id=1, source_target_pairs={{0,1},{1,0},{2,3},{3,2},{4,5},{5,4},{6,7},{7,6},{8,9},{9,8},{10,11... | collective-permute-start | bytes 3145736 | tf_op jit(solution)/shard_map/ppermute | solution.py:200
  50.7 2.8 %attend_own.1 = (f32[8,136,256]{2,1,0:T(8,128)S(1)}, f32[8,1,256]{2,1,0:T(1,128)S(1)}) custom-call(s32[2,136]{1,0:T(2,128)S(1)} %plan.1.pairs_ref, bf16[8,128,256]{2,1,0:T(8,128)(2,1)S(1)} %bitcast.8, bf16[16,128,256]{2,1,0:T(8,128)(2,1)S(1)} %bitcast.7), custom_call_target="tpu_custom_call" | custom-call | flops 4294967296 | bytes 4194304 | tf_op jit(solution)/shard_map/attend_own/pallas_call | solution.py:203
  53.5 0.0 collective-permute-done.kv_ref
  53.5 3.8 %attend_other.1 = bf16[8,136,256]{2,1,0:T(8,128)(2,1)S(1)} custom-call(s32[2,136]{1,0:T(2,128)S(1)} %plan.1.pairs_ref, bf16[8,128,256]{2,1,0:T(8,128)(2,1)S(1)} %bitcast.9, bf16[16,128,256]{2,1,0:T(8,128)(2,1)S(1)} %collective-permute-done.kv_ref, f32[8,136,256]{2,1,0:T(8,128)S(1)} %get-tuple-element.17.refs_0_, f32[8,1,256]{2,1,0:T(1,128)S(1)} %get-tuple-element.18.refs_1_), custom_call_target="tpu_custom_call" | custom-call | flops 4294967296 | bytes 4194304 | tf_op jit(solution)/shard_map/attend_other/pallas_call | solution.py:212
  57.3 17.4 %all_to_all.10.parts_ref = bf16[8,136,256]{2,1,0:T(8,128)(2,1)S(1)} all-to-all(bf16[8,136,256]{2,1,0:T(8,128)(2,1)S(1)} %attend_other.1), channel_id=1, replica_groups=mesh['zl'=2,'yh'=4,'yl'=2,'zh'=4,'x'=4,'core'=2] {'zl','x'}, dimensions={0} | all-to-all | bytes 1114112 | tf_op jit(solution)/shard_map/all_to_all | solution.py:221
  74.7 0.9 %merge.1 = f32[64,512]{1,0:T(8,128)} custom-call(bf16[8,136,256]{2,1,0:T(8,128)(2,1)S(1)} %all_to_all.10.parts_ref), custom_call_target="tpu_custom_call" | custom-call | bytes 4194304 | tf_op jit(solution)/shard_map/merge/pallas_call | solution.py:222
  (2 shorter events, 0.0 us)
Async XLA Ops:
  1.8 15.6 %copy-start = (bf16[64,512]{1,0:T(8,128)(2,1)S(1)}, bf16[64,512]{1,0:T(8,128)(2,1)}, u32[]{:S(2)}) copy-start(bf16[64,512]{1,0:T(8,128)(2,1)} %rows_ref.1) | copy-start | bytes 196612
  1.8 15.7 %copy-start.1 = (s32[256,256]{1,0:T(8,128)S(1)}, s32[256,256]{1,0:T(8,128)}, u32[]{:S(2)}) copy-start(s32[256,256]{1,0:T(8,128)} %param.7) | copy-start | bytes 786436
  1.8 46.9 %all-to-all-start = ((bf16[32,64,256]{2,1,0:T(8,128)(2,1)}), bf16[32,64,256]{2,1,0:T(8,128)(2,1)S(1)}, u32[]{:S(2)}, u32[]{:S(2)}) async-start(bf16[32,64,256]{2,1,0:T(8,128)(2,1)} %broadcast_in_dim.2), calls=%async_computation | async-start | bytes 2097152 | tf_op jit(solution)/shard_map/all_to_all | solution.py:176
  48.8 4.8 %collective-permute-start = (bf16[16,128,256]{2,1,0:T(8,128)(2,1)S(1)}, bf16[16,128,256]{2,1,0:T(8,128)(2,1)S(1)}, u32[]{:S(2)}, u32[]{:S(2)}) collective-permute-start(bf16[16,128,256]{2,1,0:T(8,128)(2,1)S(1)} %bitcast.6), channel_id=1, source_target_pairs={{0,1},{1,0},{2,3},{3,2},{4,5},{5,4},{6,7},{7,6},{8,9},{9,8},{10,11... | collective-permute-start | bytes 3145736 | tf_op jit(solution)/shard_map/ppermute | solution.py:200

commit v8 on v7

--- a/solution.py
+++ b/solution.py
@@ -19,7 +19,7 @@
 
 AXES = ("zl", "yh", "yl", "zh", "x", "core")
 SIZES = (2, 4, 2, 4, 4, 2)
-Q_AXES = ("zl", "x")
+Q_AXES = ("x", "zl")
 KV_AXES = ("zh", "yh", "yl")
 N_OWN = 8
 N_KB = 16
@@ -43,9 +43,10 @@
         full, diag = jnp.int32(0), jnp.int32(0)
         for i in range(N_PAIR):
             kb, own = i // N_OWN, i % N_OWN
+            row = (zl + own % 2) % 2 * 4 + own // 2
             key_block = k_base + (kb // 4) * 64 + kb % 4
-            query_block = q_base + (own // 4) * 128 + own % 4
-            listed = table_ref[own, key_block]
+            query_block = q_base + (row // 4) * 128 + row % 4
+            listed = table_ref[row, key_block]
             on_diag = jnp.where(key_block == query_block, listed, 0)
             pairs_ref[side, 2 + full] = jnp.int32(i)
             pairs_ref[side, LIST - 1 - diag] = jnp.int32(i)
@@ -55,9 +56,10 @@
         pairs_ref[side, 1] = diag
 
 
-def turn_kernel(rows_ref, out_ref):
-    heads = [rows_ref[:, h * DH : (h + 1) * DH] for h in range(H)]
-    out_ref[...] = jnp.concatenate(heads, axis=0).T
+def turn_kernel(own_ref, other_ref, out_ref):
+    for side, rows_ref in enumerate((own_ref, other_ref)):
+        heads = [rows_ref[:, h * DH : (h + 1) * DH] for h in range(H)]
+        out_ref[side] = jnp.concatenate(heads, axis=0).T
 
 
 def split3(x):
@@ -130,10 +132,11 @@
 
     for own in range(N_OWN):
         acc = acc_ref[own]
-        out_ref[own, :DH, :] = acc[:DH].astype(BF16)
+        to = own // 2 * 2 + (own + lax.axis_index("zl")) % 2
+        out_ref[to, :DH, :] = acc[:DH].astype(BF16)
         fill = jnp.zeros((EXT - DH - 6, COLS), BF16)
         pieces = (*split3(acc[DH : DH + 1]), *split3(top_ref[own]), fill)
-        out_ref[own, DH:, :] = jnp.concatenate(pieces, axis=0)
+        out_ref[to, DH:, :] = jnp.concatenate(pieces, axis=0)
 
 
 def merge_kernel(parts_ref, out_ref):
@@ -171,14 +174,21 @@
 
 
 def shards(queries, keys, values, block_mask):
+    other = lax.ppermute(queries, "zl", [(0, 1), (1, 0)])
     kv = jnp.concatenate((keys, values), axis=1)
     kv = jnp.broadcast_to(kv[None], (2 * N_KB, ROWS, 2 * DH))
     kv = lax.all_to_all(kv, KV_AXES, split_axis=0, concat_axis=0, tiled=True)
     kv = kv.reshape(N_KB, BLOCK, 2 * DH)
 
+    turned = call(
+        turn_kernel, "turn", jax.ShapeDtypeStruct((2, DH, COLS), BF16), [VMEM] * 2
+    )(queries, other)
+    gathered = lax.all_gather(turned, "x", axis=0, tiled=True)
+
+    mask, gathered = lax.optimization_barrier((block_mask, gathered))
     line = (lax.axis_index("yh") * 2 + lax.axis_index("yl")) * 4 + lax.axis_index("zh")
     table = lax.dynamic_index_in_dim(
-        block_mask.reshape(2, 32, 4, 256), line, 1, keepdims=False
+        mask.reshape(2, 32, 4, 256), line, 1, keepdims=False
     ).reshape(N_OWN, 256)
     pairs = call(
         plan_kernel,
@@ -186,14 +196,9 @@
         jax.ShapeDtypeStruct((2, LIST), jnp.int32),
         [SMEM],
         out_specs=SMEM,
+        flops=64 << 30,
     )(table)
 
-    turned = call(
-        turn_kernel, "turn", jax.ShapeDtypeStruct((DH, COLS), BF16), [VMEM]
-    )(queries)
-    gathered = lax.all_gather(turned, "x", axis=0, tiled=True)
-    gathered, pairs = lax.optimization_barrier((gathered, pairs))
-    gathered = lax.all_gather(gathered, "zl", axis=0, tiled=True)
     gathered = gathered.reshape(N_OWN, DH, COLS)
 
     kv, gathered, pairs = lax.optimization_barrier((kv, gathered, pairs))

time: 75.4 us -> 76.4 us (1.013)
  the two profiles are of different devices: /device:TPU:56 before, /device:TPU:24 now
where the time goes in v8:
time: 76.4 us; the launch traced here: 76 us
  blocking collectives  30.1 us (39%)
  starting transfers between devices  21.4 us (28%)
  waiting for transfers between devices  13.2 us (17%)
  Pallas kernels  9.27 us (12%)
  local copies, waits for them, and re-layouts  1.19 us (2%)
    all_to_all x1, blocking collectives, shards(): lax.all_to_all(parts, Q_AXES, split_axis=0, concat_axis=0, tiled=True)  17 us
    all_to_all x1, starting transfers between devices, shards(): kv = lax.all_to_all(kv, KV_AXES, split_axis=0, concat_axis=0, tiled=True)  15.2 us
    all_gather x1, blocking collectives, shards(): gathered = lax.all_gather(turned, 'x', axis=0, tiled=True)  13.1 us
    all_to_all x1, waiting for transfers between devices, shards(): kv = lax.all_to_all(kv, KV_AXES, split_axis=0, concat_axis=0, tiled=True)  13.1 us
    ppermute x1, starting transfers between devices, shards(): other = lax.ppermute(queries, 'zl', [(0, 1), (1, 0)])  4.27 us
    pallas_call x1, Pallas kernels, shards(): call(plan_kernel, 'plan', jax.ShapeDtypeStruct((2, LIST), jnp.int32), [SM...  3.39 us
    pallas_call x1, Pallas kernels, shards(): call(functools.partial(attend_kernel, 0), 'attend_own', (jax.ShapeDtypeSt...  2.5 us
    pallas_call x1, Pallas kernels, shards(): call(functools.partial(attend_kernel, 1), 'attend_other', jax.ShapeDtypeS...  2.43 us
  transfers between devices with their start and end apart: 3, of which 2 were waited for; matrix products, arithmetic and copies ran while one was open for 3% of the time, Pallas kernels for 8%

profile of v8, /device:TPU:24, one launch (start us, length us, event | category | flops | bytes accessed | tf_op | source)
XLA Modules:
  0.0 76.0 jit_solution(11263465983706146683)
XLA Ops:
  0.0 4.3 %collective-permute-start = (bf16[64,512]{1,0:T(8,128)(2,1)}, bf16[64,512]{1,0:T(8,128)(2,1)S(1)}, u32[]{:S(2)}, u32[]{:S(2)}) collective-permute-start(bf16[64,512]{1,0:T(8,128)(2,1)} %own_ref.1), channel_id=1, source_target_pairs={{0,256},{256,0},{1,257},{257,1},{2,258},{258,2},{3,259},{259,3},{4... | collective-permute-start | bytes 196616 | tf_op jit(solution)/shard_map/ppermute | solution.py:177
  4.3 0.7 pad_maximum_fusion
  5.0 1.1 %broadcast_in_dim.2 = bf16[32,64,256]{2,1,0:T(8,128)(2,1)} broadcast(bf16[64,256]{1,0:T(8,128)(2,1)S(1)} %pad_maximum_fusion), dimensions={1,2} | broadcast | bytes 1081344 | tf_op jit(solution)/shard_map/broadcast_in_dim | solution.py:179
  6.1 0.0 copy-start
  6.1 0.0 copy-start.1
  6.1 15.2 %all-to-all-start = ((bf16[32,64,256]{2,1,0:T(8,128)(2,1)}), bf16[32,64,256]{2,1,0:T(8,128)(2,1)S(1)}, u32[]{:S(2)}, u32[]{:S(2)}) async-start(bf16[32,64,256]{2,1,0:T(8,128)(2,1)} %broadcast_in_dim.2), calls=%async_computation | async-start | bytes 2097152 | tf_op jit(solution)/shard_map/all_to_all | solution.py:180
  21.3 0.0 collective-permute-done.other_ref
  21.3 0.0 copy-done
  21.3 0.1 turn.1
  21.4 13.1 %all_gather.3.q_ref = bf16[8,128,256]{2,1,0:T(8,128)(2,1)S(1)} all-gather(bf16[2,128,256]{2,1,0:T(8,128)(2,1)S(1)} %turn.1), channel_id=1, replica_groups=mesh['zl'=2,'yh'=4,'yl'=2,'zh'=4,'x'=4,'core'=2] {'x'}, dimensions={0}, use_global_device_ids=true | all-gather | bytes 655360 | tf_op jit(solution)/shard_map/all_gather | solution.py:186
  34.6 0.0 copy-done.1
  34.6 0.1 reshape.12
  34.7 3.4 %plan.1.pairs_ref = s32[2,136]{1,0:T(2,128)S(1)} custom-call(s32[8,256]{1,0:T(8,128)S(1)} %reshape.13.table_ref), custom_call_target="tpu_custom_call" | custom-call | flops 68719476736 | bytes 4194304 | tf_op jit(solution)/shard_map/plan/pallas_call | solution.py:193
  38.1 13.1 %all-to-all-done = bf16[32,64,256]{2,1,0:T(8,128)(2,1)S(1)} async-done(((bf16[32,64,256]{2,1,0:T(8,128)(2,1)}), bf16[32,64,256]{2,1,0:T(8,128)(2,1)S(1)}, u32[]{:S(2)}, u32[]{:S(2)}) %all-to-all-start) | async-done | bytes 1048608 | tf_op jit(solution)/shard_map/all_to_all | solution.py:180
  51.2 1.9 %collective-permute-start.1 = (bf16[16,128,256]{2,1,0:T(8,128)(2,1)S(1)}, bf16[16,128,256]{2,1,0:T(8,128)(2,1)S(1)}, u32[]{:S(2)}, u32[]{:S(2)}) collective-permute-start(bf16[16,128,256]{2,1,0:T(8,128)(2,1)S(1)} %bitcast.5), channel_id=1, source_target_pairs={{0,1},{1,0},{2,3},{3,2},{4,5},{5,4},{6,7},{7,6},{8,9},{9,8},{10,11... | collective-permute-start | bytes 3145736 | tf_op jit(solution)/shard_map/ppermute | solution.py:205
  53.1 2.5 %attend_own.1 = (f32[8,136,256]{2,1,0:T(8,128)S(1)}, f32[8,1,256]{2,1,0:T(1,128)S(1)}) custom-call(s32[2,136]{1,0:T(2,128)S(1)} %plan.1.pairs_ref, bf16[8,128,256]{2,1,0:T(8,128)(2,1)S(1)} %all_gather.3.q_ref, bf16[16,128,256]{2,1,0:T(8,128)(2,1)S(1)} %bitcast.6), custom_call_target="tpu_custom_call" | custom-call | flops 4294967296 | bytes 4194304 | tf_op jit(solution)/shard_map/attend_own/pallas_call | solution.py:208
  55.6 0.1 collective-permute-done.1.kv_ref
  55.7 2.4 %attend_other.1 = bf16[8,136,256]{2,1,0:T(8,128)(2,1)S(1)} custom-call(s32[2,136]{1,0:T(2,128)S(1)} %plan.1.pairs_ref, bf16[8,128,256]{2,1,0:T(8,128)(2,1)S(1)} %all_gather.3.q_ref, bf16[16,128,256]{2,1,0:T(8,128)(2,1)S(1)} %collective-permute-done.1.kv_ref, f32[8,136,256]{2,1,0:T(8,128)S(1)} %get-tuple-element.17.refs_0_, ...), custom_call_target="tpu_custom_call" | custom-call | flops 4294967296 | bytes 4194304 | tf_op jit(solution)/shard_map/attend_other/pallas_call | solution.py:217
  58.1 17.0 %all_to_all.10.parts_ref = bf16[8,136,256]{2,1,0:T(8,128)(2,1)S(1)} all-to-all(bf16[8,136,256]{2,1,0:T(8,128)(2,1)S(1)} %attend_other.1), channel_id=1, replica_groups=mesh['zl'=2,'yh'=4,'yl'=2,'zh'=4,'x'=4,'core'=2] {'x','zl'}, dimensions={0} | all-to-all | bytes 1114112 | tf_op jit(solution)/shard_map/all_to_all | solution.py:226
  75.1 0.9 %merge.1 = f32[64,512]{1,0:T(8,128)} custom-call(bf16[8,136,256]{2,1,0:T(8,128)(2,1)S(1)} %all_to_all.10.parts_ref), custom_call_target="tpu_custom_call" | custom-call | bytes 4194304 | tf_op jit(solution)/shard_map/merge/pallas_call | solution.py:227
  (2 shorter events, 0.0 us)
Async XLA Ops:
  0.0 21.3 %collective-permute-start = (bf16[64,512]{1,0:T(8,128)(2,1)}, bf16[64,512]{1,0:T(8,128)(2,1)S(1)}, u32[]{:S(2)}, u32[]{:S(2)}) collective-permute-start(bf16[64,512]{1,0:T(8,128)(2,1)} %own_ref.1), channel_id=1, source_target_pairs={{0,256},{256,0},{1,257},{257,1},{2,258},{258,2},{3,259},{259,3},{4... | collective-permute-start | bytes 196616 | tf_op jit(solution)/shard_map/ppermute | solution.py:177
  6.1 15.2 %copy-start = (bf16[64,512]{1,0:T(8,128)(2,1)S(1)}, bf16[64,512]{1,0:T(8,128)(2,1)}, u32[]{:S(2)}) copy-start(bf16[64,512]{1,0:T(8,128)(2,1)} %own_ref.1) | copy-start | bytes 196612
  6.1 28.4 %copy-start.1 = (s32[256,256]{1,0:T(8,128)S(1)}, s32[256,256]{1,0:T(8,128)}, u32[]{:S(2)}) copy-start(s32[256,256]{1,0:T(8,128)} %param.7) | copy-start | bytes 786436
  6.1 45.1 %all-to-all-start = ((bf16[32,64,256]{2,1,0:T(8,128)(2,1)}), bf16[32,64,256]{2,1,0:T(8,128)(2,1)S(1)}, u32[]{:S(2)}, u32[]{:S(2)}) async-start(bf16[32,64,256]{2,1,0:T(8,128)(2,1)} %broadcast_in_dim.2), calls=%async_computation | async-start | bytes 2097152 | tf_op jit(solution)/shard_map/all_to_all | solution.py:180
  51.2 4.5 %collective-permute-start.1 = (bf16[16,128,256]{2,1,0:T(8,128)(2,1)S(1)}, bf16[16,128,256]{2,1,0:T(8,128)(2,1)S(1)}, u32[]{:S(2)}, u32[]{:S(2)}) collective-permute-start(bf16[16,128,256]{2,1,0:T(8,128)(2,1)S(1)} %bitcast.5), channel_id=1, source_target_pairs={{0,1},{1,0},{2,3},{3,2},{4,5},{5,4},{6,7},{7,6},{8,9},{9,8},{10,11... | collective-permute-start | bytes 3145736 | tf_op jit(solution)/shard_map/ppermute | solution.py:205

commit v9 on v7

--- a/solution.py
+++ b/solution.py
@@ -25,7 +25,7 @@
 N_KB = 16
 N_PAIR = N_OWN * N_KB
 LIST = N_PAIR + 8
-WIDTHS = (12, 4, 2, 1)
+WIDTHS = ((12, 6, 3, 2, 1), (16, 8, 4, 2, 1))
 DIAGONAL_WIDTHS = (8, 1)
 EXT = DH + 8
 
@@ -123,7 +123,7 @@
 
             done = lax.fori_loop(0, (count - done) // width, several, done)
 
-    run(full, WIDTHS, lambda at: pairs_ref[side, 2 + at], False)
+    run(full, WIDTHS[side], lambda at: pairs_ref[side, 2 + at], False)
     run(diag, DIAGONAL_WIDTHS, lambda at: pairs_ref[side, LIST - 1 - at], True)
     if side == 0:
         return

time: 75.4 us -> 74.7 us (level)
  blocking collectives: 45.4 us -> 44.1 us
    all_to_all x1, blocking collectives: 17.4 us -> 16.1 us  [shards(): lax.all_to_all(parts, Q_AXES, split_axis=0, concat_axis=0, tiled=True)]
where the time goes in v9:
time: 74.7 us; the launch traced here: 74.3 us
  blocking collectives  44.1 us (59%)
  starting transfers between devices  17.5 us (23%)
  Pallas kernels  10.6 us (14%)
  local copies, waits for them, and re-layouts  1.2 us (2%)
    all_to_all x1, blocking collectives, shards(): lax.all_to_all(parts, Q_AXES, split_axis=0, concat_axis=0, tiled=True)  16.1 us
    all_to_all x1, starting transfers between devices, shards(): kv = lax.all_to_all(kv, KV_AXES, split_axis=0, concat_axis=0, tiled=True)  15.6 us
    all_gather x1, blocking collectives, shards(): gathered = lax.all_gather(gathered, 'zl', axis=0, tiled=True)  15.4 us
    all_gather x1, blocking collectives, shards(): gathered = lax.all_gather(turned, 'x', axis=0, tiled=True)  12.6 us
    pallas_call x1, Pallas kernels, shards(): call(functools.partial(attend_kernel, 1), 'attend_other', jax.ShapeDtypeS...  3.84 us
    pallas_call x1, Pallas kernels, shards(): call(plan_kernel, 'plan', jax.ShapeDtypeStruct((2, LIST), jnp.int32), [SM...  3.05 us
    pallas_call x1, Pallas kernels, shards(): call(functools.partial(attend_kernel, 0), 'attend_own', (jax.ShapeDtypeSt...  2.81 us
    ppermute x1, starting transfers between devices, shards(): kv_other = lax.ppermute(kv, 'core', [(0, 1), (1, 0)])  1.91 us
  transfers between devices with their start and end apart: 2, of which 0 were waited for; matrix products, arithmetic and copies ran while one was open for 0% of the time, Pallas kernels for 8%

profile of v9, /device:TPU:56, one launch (start us, length us, event | category | flops | bytes accessed | tf_op | source)
XLA Modules:
  0.0 74.3 jit_solution(11699393760445625242)
XLA Ops:
  0.0 0.7 pad_maximum_fusion
  0.7 1.1 %broadcast_in_dim.2 = bf16[32,64,256]{2,1,0:T(8,128)(2,1)} broadcast(bf16[64,256]{1,0:T(8,128)(2,1)S(1)} %pad_maximum_fusion), dimensions={1,2} | broadcast | bytes 1081344 | tf_op jit(solution)/shard_map/broadcast_in_dim | solution.py:175
  1.8 0.0 copy-start
  1.8 0.0 copy-start.1
  1.8 15.6 %all-to-all-start = ((bf16[32,64,256]{2,1,0:T(8,128)(2,1)}), bf16[32,64,256]{2,1,0:T(8,128)(2,1)S(1)}, u32[]{:S(2)}, u32[]{:S(2)}) async-start(bf16[32,64,256]{2,1,0:T(8,128)(2,1)} %broadcast_in_dim.2), calls=%async_computation | async-start | bytes 2097152 | tf_op jit(solution)/shard_map/all_to_all | solution.py:176
  17.5 0.0 copy-done
  17.5 0.1 turn.1
  17.6 0.0 copy-done.1
  17.6 0.1 reshape.15
  17.7 3.1 %plan.1.pairs_ref = s32[2,136]{1,0:T(2,128)S(1)} custom-call(s32[8,256]{1,0:T(8,128)S(1)} %reshape.16.table_ref), custom_call_target="tpu_custom_call" | custom-call | bytes 4194304 | tf_op jit(solution)/shard_map/plan/pallas_call | solution.py:183
  20.7 12.6 %all_gather.6 = bf16[512,256]{1,0:T(8,128)(2,1)S(1)} all-gather(bf16[128,256]{1,0:T(8,128)(2,1)S(1)} %turn.1), channel_id=1, replica_groups=mesh['zl'=2,'yh'=4,'yl'=2,'zh'=4,'x'=4,'core'=2] {'x'}, dimensions={0}, use_global_device_ids=true | all-gather | bytes 327680 | tf_op jit(solution)/shard_map/all_gather | solution.py:194
  33.4 15.4 %all_gather.7 = bf16[1024,256]{1,0:T(8,128)(2,1)S(1)} all-gather(bf16[512,256]{1,0:T(8,128)(2,1)S(1)} %all_gather.6), channel_id=1, replica_groups=mesh['zl'=2,'yh'=4,'yl'=2,'zh'=4,'x'=4,'core'=2] {'zl'}, dimensions={0}, use_global_device_ids=true | all-gather | bytes 786432 | tf_op jit(solution)/shard_map/all_gather | solution.py:196
  48.8 0.0 all-to-all-done
  48.8 1.9 %collective-permute-start = (bf16[16,128,256]{2,1,0:T(8,128)(2,1)S(1)}, bf16[16,128,256]{2,1,0:T(8,128)(2,1)S(1)}, u32[]{:S(2)}, u32[]{:S(2)}) collective-permute-start(bf16[16,128,256]{2,1,0:T(8,128)(2,1)S(1)} %bitcast.6), channel_id=1, source_target_pairs={{0,1},{1,0},{2,3},{3,2},{4,5},{5,4},{6,7},{7,6},{8,9},{9,8},{10,11... | collective-permute-start | bytes 3145736 | tf_op jit(solution)/shard_map/ppermute | solution.py:200
  50.7 2.8 %attend_own.1 = (f32[8,136,256]{2,1,0:T(8,128)S(1)}, f32[8,1,256]{2,1,0:T(1,128)S(1)}) custom-call(s32[2,136]{1,0:T(2,128)S(1)} %plan.1.pairs_ref, bf16[8,128,256]{2,1,0:T(8,128)(2,1)S(1)} %bitcast.8, bf16[16,128,256]{2,1,0:T(8,128)(2,1)S(1)} %bitcast.7), custom_call_target="tpu_custom_call" | custom-call | flops 4294967296 | bytes 4194304 | tf_op jit(solution)/shard_map/attend_own/pallas_call | solution.py:203
  53.5 0.0 collective-permute-done.kv_ref
  53.5 3.8 %attend_other.1 = bf16[8,136,256]{2,1,0:T(8,128)(2,1)S(1)} custom-call(s32[2,136]{1,0:T(2,128)S(1)} %plan.1.pairs_ref, bf16[8,128,256]{2,1,0:T(8,128)(2,1)S(1)} %bitcast.9, bf16[16,128,256]{2,1,0:T(8,128)(2,1)S(1)} %collective-permute-done.kv_ref, f32[8,136,256]{2,1,0:T(8,128)S(1)} %get-tuple-element.17.refs_0_, f32[8,1,256]{2,1,0:T(1,128)S(1)} %get-tuple-element.18.refs_1_), custom_call_target="tpu_custom_call" | custom-call | flops 4294967296 | bytes 4194304 | tf_op jit(solution)/shard_map/attend_other/pallas_call | solution.py:212
  57.4 16.1 %all_to_all.10.parts_ref = bf16[8,136,256]{2,1,0:T(8,128)(2,1)S(1)} all-to-all(bf16[8,136,256]{2,1,0:T(8,128)(2,1)S(1)} %attend_other.1), channel_id=1, replica_groups=mesh['zl'=2,'yh'=4,'yl'=2,'zh'=4,'x'=4,'core'=2] {'zl','x'}, dimensions={0} | all-to-all | bytes 1114112 | tf_op jit(solution)/shard_map/all_to_all | solution.py:221
  73.4 0.9 %merge.1 = f32[64,512]{1,0:T(8,128)} custom-call(bf16[8,136,256]{2,1,0:T(8,128)(2,1)S(1)} %all_to_all.10.parts_ref), custom_call_target="tpu_custom_call" | custom-call | bytes 4194304 | tf_op jit(solution)/shard_map/merge/pallas_call | solution.py:222
  (2 shorter events, 0.0 us)
Async XLA Ops:
  1.8 15.6 %copy-start = (bf16[64,512]{1,0:T(8,128)(2,1)S(1)}, bf16[64,512]{1,0:T(8,128)(2,1)}, u32[]{:S(2)}) copy-start(bf16[64,512]{1,0:T(8,128)(2,1)} %rows_ref.1) | copy-start | bytes 196612
  1.8 15.7 %copy-start.1 = (s32[256,256]{1,0:T(8,128)S(1)}, s32[256,256]{1,0:T(8,128)}, u32[]{:S(2)}) copy-start(s32[256,256]{1,0:T(8,128)} %param.7) | copy-start | bytes 786436
  1.8 46.9 %all-to-all-start = ((bf16[32,64,256]{2,1,0:T(8,128)(2,1)}), bf16[32,64,256]{2,1,0:T(8,128)(2,1)S(1)}, u32[]{:S(2)}, u32[]{:S(2)}) async-start(bf16[32,64,256]{2,1,0:T(8,128)(2,1)} %broadcast_in_dim.2), calls=%async_computation | async-start | bytes 2097152 | tf_op jit(solution)/shard_map/all_to_all | solution.py:176
  48.8 4.7 %collective-permute-start = (bf16[16,128,256]{2,1,0:T(8,128)(2,1)S(1)}, bf16[16,128,256]{2,1,0:T(8,128)(2,1)S(1)}, u32[]{:S(2)}, u32[]{:S(2)}) collective-permute-start(bf16[16,128,256]{2,1,0:T(8,128)(2,1)S(1)} %bitcast.6), channel_id=1, source_target_pairs={{0,1},{1,0},{2,3},{3,2},{4,5},{5,4},{6,7},{7,6},{8,9},{9,8},{10,11... | collective-permute-start | bytes 3145736 | tf_op jit(solution)/shard_map/ppermute | solution.py:200

commit v10 on v7

--- a/solution.py
+++ b/solution.py
@@ -25,7 +25,7 @@
 N_KB = 16
 N_PAIR = N_OWN * N_KB
 LIST = N_PAIR + 8
-WIDTHS = (12, 4, 2, 1)
+WIDTHS = (14, 7, 3, 1)
 DIAGONAL_WIDTHS = (8, 1)
 EXT = DH + 8
 

time: 75.4 us -> 75.4 us (level)
  blocking collectives: 45.4 us -> 44.6 us
    all_to_all x1, blocking collectives: 17.4 us -> 16.6 us  [shards(): lax.all_to_all(parts, Q_AXES, split_axis=0, concat_axis=0, tiled=True)]
  transfers between devices with their start and end apart: 2 -> 2, of which waited for: 0 -> 0; matrix products, arithmetic and copies ran while one was open for 0% -> 0% of each run, Pallas kernels for 8% -> 9%
where the time goes in v10:
time: 75.4 us; the launch traced here: 74.8 us
  blocking collectives  44.6 us (59%)
  starting transfers between devices  17.5 us (23%)
  Pallas kernels  10.6 us (14%)
  local copies, waits for them, and re-layouts  1.2 us (2%)
    all_to_all x1, blocking collectives, shards(): lax.all_to_all(parts, Q_AXES, split_axis=0, concat_axis=0, tiled=True)  16.6 us
    all_to_all x1, starting transfers between devices, shards(): kv = lax.all_to_all(kv, KV_AXES, split_axis=0, concat_axis=0, tiled=True)  15.6 us
    all_gather x1, blocking collectives, shards(): gathered = lax.all_gather(gathered, 'zl', axis=0, tiled=True)  15.4 us
    all_gather x1, blocking collectives, shards(): gathered = lax.all_gather(turned, 'x', axis=0, tiled=True)  12.6 us
    pallas_call x1, Pallas kernels, shards(): call(functools.partial(attend_kernel, 0), 'attend_own', (jax.ShapeDtypeSt...  3.49 us
    pallas_call x1, Pallas kernels, shards(): call(functools.partial(attend_kernel, 1), 'attend_other', jax.ShapeDtypeS...  3.16 us
    pallas_call x1, Pallas kernels, shards(): call(plan_kernel, 'plan', jax.ShapeDtypeStruct((2, LIST), jnp.int32), [SM...  3.05 us
    ppermute x1, starting transfers between devices, shards(): kv_other = lax.ppermute(kv, 'core', [(0, 1), (1, 0)])  1.91 us
  transfers between devices with their start and end apart: 2, of which 0 were waited for; matrix products, arithmetic and copies ran while one was open for 0% of the time, Pallas kernels for 9%

profile of v10, /device:TPU:56, one launch (start us, length us, event | category | flops | bytes accessed | tf_op | source)
XLA Modules:
  0.0 74.8 jit_solution(10421844979162871568)
XLA Ops:
  0.0 0.7 pad_maximum_fusion
  0.7 1.1 %broadcast_in_dim.2 = bf16[32,64,256]{2,1,0:T(8,128)(2,1)} broadcast(bf16[64,256]{1,0:T(8,128)(2,1)S(1)} %pad_maximum_fusion), dimensions={1,2} | broadcast | bytes 1081344 | tf_op jit(solution)/shard_map/broadcast_in_dim | solution.py:175
  1.8 0.0 copy-start
  1.8 0.0 copy-start.1
  1.8 15.6 %all-to-all-start = ((bf16[32,64,256]{2,1,0:T(8,128)(2,1)}), bf16[32,64,256]{2,1,0:T(8,128)(2,1)S(1)}, u32[]{:S(2)}, u32[]{:S(2)}) async-start(bf16[32,64,256]{2,1,0:T(8,128)(2,1)} %broadcast_in_dim.2), calls=%async_computation | async-start | bytes 2097152 | tf_op jit(solution)/shard_map/all_to_all | solution.py:176
  17.5 0.0 copy-done
  17.5 0.1 turn.1
  17.6 0.0 copy-done.1
  17.6 0.1 reshape.15
  17.7 3.1 %plan.1.pairs_ref = s32[2,136]{1,0:T(2,128)S(1)} custom-call(s32[8,256]{1,0:T(8,128)S(1)} %reshape.16.table_ref), custom_call_target="tpu_custom_call" | custom-call | bytes 4194304 | tf_op jit(solution)/shard_map/plan/pallas_call | solution.py:183
  20.7 12.6 %all_gather.6 = bf16[512,256]{1,0:T(8,128)(2,1)S(1)} all-gather(bf16[128,256]{1,0:T(8,128)(2,1)S(1)} %turn.1), channel_id=1, replica_groups=mesh['zl'=2,'yh'=4,'yl'=2,'zh'=4,'x'=4,'core'=2] {'x'}, dimensions={0}, use_global_device_ids=true | all-gather | bytes 327680 | tf_op jit(solution)/shard_map/all_gather | solution.py:194
  33.4 15.4 %all_gather.7 = bf16[1024,256]{1,0:T(8,128)(2,1)S(1)} all-gather(bf16[512,256]{1,0:T(8,128)(2,1)S(1)} %all_gather.6), channel_id=1, replica_groups=mesh['zl'=2,'yh'=4,'yl'=2,'zh'=4,'x'=4,'core'=2] {'zl'}, dimensions={0}, use_global_device_ids=true | all-gather | bytes 786432 | tf_op jit(solution)/shard_map/all_gather | solution.py:196
  48.8 0.0 all-to-all-done
  48.8 1.9 %collective-permute-start = (bf16[16,128,256]{2,1,0:T(8,128)(2,1)S(1)}, bf16[16,128,256]{2,1,0:T(8,128)(2,1)S(1)}, u32[]{:S(2)}, u32[]{:S(2)}) collective-permute-start(bf16[16,128,256]{2,1,0:T(8,128)(2,1)S(1)} %bitcast.6), channel_id=1, source_target_pairs={{0,1},{1,0},{2,3},{3,2},{4,5},{5,4},{6,7},{7,6},{8,9},{9,8},{10,11... | collective-permute-start | bytes 3145736 | tf_op jit(solution)/shard_map/ppermute | solution.py:200
  50.7 3.5 %attend_own.1 = (f32[8,136,256]{2,1,0:T(8,128)S(1)}, f32[8,1,256]{2,1,0:T(1,128)S(1)}) custom-call(s32[2,136]{1,0:T(2,128)S(1)} %plan.1.pairs_ref, bf16[8,128,256]{2,1,0:T(8,128)(2,1)S(1)} %bitcast.8, bf16[16,128,256]{2,1,0:T(8,128)(2,1)S(1)} %bitcast.7), custom_call_target="tpu_custom_call" | custom-call | flops 4294967296 | bytes 4194304 | tf_op jit(solution)/shard_map/attend_own/pallas_call | solution.py:203
  54.2 0.0 collective-permute-done.kv_ref
  54.2 3.2 %attend_other.1 = bf16[8,136,256]{2,1,0:T(8,128)(2,1)S(1)} custom-call(s32[2,136]{1,0:T(2,128)S(1)} %plan.1.pairs_ref, bf16[8,128,256]{2,1,0:T(8,128)(2,1)S(1)} %bitcast.9, bf16[16,128,256]{2,1,0:T(8,128)(2,1)S(1)} %collective-permute-done.kv_ref, f32[8,136,256]{2,1,0:T(8,128)S(1)} %get-tuple-element.17.refs_0_, f32[8,1,256]{2,1,0:T(1,128)S(1)} %get-tuple-element.18.refs_1_), custom_call_target="tpu_custom_call" | custom-call | flops 4294967296 | bytes 4194304 | tf_op jit(solution)/shard_map/attend_other/pallas_call | solution.py:212
  57.4 16.6 %all_to_all.10.parts_ref = bf16[8,136,256]{2,1,0:T(8,128)(2,1)S(1)} all-to-all(bf16[8,136,256]{2,1,0:T(8,128)(2,1)S(1)} %attend_other.1), channel_id=1, replica_groups=mesh['zl'=2,'yh'=4,'yl'=2,'zh'=4,'x'=4,'core'=2] {'zl','x'}, dimensions={0} | all-to-all | bytes 1114112 | tf_op jit(solution)/shard_map/all_to_all | solution.py:221
  74.0 0.9 %merge.1 = f32[64,512]{1,0:T(8,128)} custom-call(bf16[8,136,256]{2,1,0:T(8,128)(2,1)S(1)} %all_to_all.10.parts_ref), custom_call_target="tpu_custom_call" | custom-call | bytes 4194304 | tf_op jit(solution)/shard_map/merge/pallas_call | solution.py:222
  (2 shorter events, 0.0 us)
Async XLA Ops:
  1.8 15.6 %copy-start = (bf16[64,512]{1,0:T(8,128)(2,1)S(1)}, bf16[64,512]{1,0:T(8,128)(2,1)}, u32[]{:S(2)}) copy-start(bf16[64,512]{1,0:T(8,128)(2,1)} %rows_ref.1) | copy-start | bytes 196612
  1.8 15.7 %copy-start.1 = (s32[256,256]{1,0:T(8,128)S(1)}, s32[256,256]{1,0:T(8,128)}, u32[]{:S(2)}) copy-start(s32[256,256]{1,0:T(8,128)} %param.7) | copy-start | bytes 786436
  1.8 46.9 %all-to-all-start = ((bf16[32,64,256]{2,1,0:T(8,128)(2,1)}), bf16[32,64,256]{2,1,0:T(8,128)(2,1)S(1)}, u32[]{:S(2)}, u32[]{:S(2)}) async-start(bf16[32,64,256]{2,1,0:T(8,128)(2,1)} %broadcast_in_dim.2), calls=%async_computation | async-start | bytes 2097152 | tf_op jit(solution)/shard_map/all_to_all | solution.py:176
  48.8 5.4 %collective-permute-start = (bf16[16,128,256]{2,1,0:T(8,128)(2,1)S(1)}, bf16[16,128,256]{2,1,0:T(8,128)(2,1)S(1)}, u32[]{:S(2)}, u32[]{:S(2)}) collective-permute-start(bf16[16,128,256]{2,1,0:T(8,128)(2,1)S(1)} %bitcast.6), channel_id=1, source_target_pairs={{0,1},{1,0},{2,3},{3,2},{4,5},{5,4},{6,7},{7,6},{8,9},{9,8},{10,11... | collective-permute-start | bytes 3145736 | tf_op jit(solution)/shard_map/ppermute | solution.py:200
